TPU v7x, 512 devices: a whole 4x4x16 slice. The times are simulated.
512 devices in a mesh: depth: 16 (over z_hi, x), rows: 32 (over z_lo, y, core).
Axes of the slice: x: 4, y: 4, z: 16 (z_hi: 4, z_lo: 4; z = z_hi * 4 + z_lo), core: 2. Of those that a mesh axis runs over, the one named last changes fastest.
Arguments:
- hologram: bfloat16 [4096, 4096], P('rows'), may hold values from 0.25 to 1.75
- background: bfloat16 [4096, 4096], P('rows'), may hold values from 0.5 to 2
Outputs:
- focus: float32 [4096, 4096], P('rows')
All inputs are finite; a program needn't handle non-finite values.
Results may differ from a plain program's by a relative error of at most 0.025.
Values may be sent and summed in bfloat16 or wider, within the bound.
A program may use at most 64 MiB of HBM per device.

v0:
```python
import math

import jax
import jax.numpy as jnp
from jax import lax
from jax.sharding import PartitionSpec as P

N = 4096
RADIX = 64
PL_DEV = 1


wave_number = 0.6
depth_start = 8.0
depth_step = 2.0


def padded_2(block, sides, width):
    for axis, dim in sides:
        count = lax.axis_size(axis)
        forward = [(i, i + 1) for i in range(count - 1)]
        backward = [(target, source) for source, target in forward]
        low = lax.ppermute(
            lax.slice_in_dim(block, block.shape[dim] - width, None, axis=dim), axis, forward
        )
        high = lax.ppermute(lax.slice_in_dim(block, 0, width, axis=dim), axis, backward)
        block = jnp.concatenate([low, block, high], axis=dim)
    return block


def fourier_tables(radix_size, sign_value):
    indices = jnp.arange(radix_size, dtype=jnp.int32)
    products = indices[:, None] * indices[None, :] % radix_size
    angles = products.astype(jnp.float32) * (sign_value * 2.0 * math.pi / radix_size)
    scaling = 1.0 / math.sqrt(radix_size)
    cosine_part = jnp.cos(angles) * scaling
    sine_part = jnp.sin(angles) * scaling
    matrix = jnp.stack([jnp.stack([cosine_part, -sine_part]), jnp.stack([sine_part, cosine_part])])
    return matrix.astype(jnp.bfloat16)


def twiddle_table(radix_size, sign_value):
    indices = jnp.arange(radix_size, dtype=jnp.int32)
    total = radix_size * radix_size
    products = indices[:, None] * indices[None, :] % total
    angles = products.astype(jnp.float32) * (sign_value * 2.0 * math.pi / total)
    return (jnp.cos(angles), jnp.sin(angles))


def rotate(data, cosine_part, sine_part):
    return jnp.stack(
        [data[0] * cosine_part - data[1] * sine_part, data[0] * sine_part + data[1] * cosine_part]
    )


def contract(form, matrix, data):
    return jnp.einsum(form, matrix, data, preferred_element_type=jnp.float32)


def forward_real(data):
    batch_size = data.shape[1]
    shaped = data.reshape(RADIX, RADIX, batch_size)
    matrix = fourier_tables(RADIX, -1.0)
    cosine_part, sine_part = twiddle_table(RADIX, -1.0)
    opening = contract("oka,abm->okbm", matrix[:, 0], shaped)
    sectioned = rotate(opening, cosine_part[:, :, None], sine_part[:, :, None]).astype(jnp.bfloat16)
    closing = contract("ocjb,ckbm->okjm", matrix, sectioned)
    return closing.reshape(2, N, batch_size).astype(jnp.bfloat16)


def forward_first(data):
    batch_size = data.shape[2]
    shaped = data.reshape(2, RADIX, RADIX, batch_size)
    matrix = fourier_tables(RADIX, -1.0)
    cosine_part, sine_part = twiddle_table(RADIX, -1.0)
    opening = contract("ocka,cabm->okbm", matrix, shaped)
    sectioned = rotate(opening, cosine_part[:, :, None], sine_part[:, :, None]).astype(jnp.bfloat16)
    closing = contract("ocjb,ckbm->okjm", matrix, sectioned)
    return closing.reshape(2, N, batch_size).astype(jnp.bfloat16)


def inverse_first(data):
    batch_size = data.shape[2]
    shaped = data.reshape(2, RADIX, RADIX, batch_size)
    matrix = fourier_tables(RADIX, 1.0)
    cosine_part, sine_part = twiddle_table(RADIX, 1.0)
    opening = contract("ocbj,ckjm->okbm", matrix, shaped)
    sectioned = rotate(opening, cosine_part[:, :, None], sine_part[:, :, None]).astype(jnp.bfloat16)
    closing = contract("ocak,ckbm->oabm", matrix, sectioned)
    return closing.reshape(2, N, batch_size)


def frequencies(positions):
    natural = positions // RADIX + RADIX * (positions % RADIX)
    signed_freq = jnp.where(natural >= N // 2, natural - N, natural)
    return signed_freq.astype(jnp.float32) / N


def propagator(freq_whole, freq_own, distance):
    radial = freq_whole[:, None] ** 2 + freq_own[None, :] ** 2
    limit = wave_number * wave_number
    amplitude = jnp.exp(-2.0 * math.pi * distance * jnp.sqrt(jnp.maximum(radial - limit, 0.0)))
    phase_angle = (
        2.0 * math.pi * distance * (jnp.sqrt(jnp.maximum(limit - radial, 0.0)) - wave_number)
    )
    return (amplitude * jnp.cos(phase_angle), amplitude * jnp.sin(phase_angle))


def propagate(spectrum, cosine_part, sine_part):
    return rotate(spectrum.astype(jnp.float32), cosine_part, sine_part).astype(jnp.bfloat16)


def shards(hologram, background):
    row_count = hologram.shape[0]
    contrast = (hologram.astype(jnp.float32) / background.astype(jnp.float32) - 1.0).astype(
        jnp.bfloat16
    )
    along_rows = forward_real(contrast.T)
    columns = lax.all_to_all(
        jnp.swapaxes(along_rows, 1, 2), "rows", split_axis=2, concat_axis=1, tiled=True
    )
    spectrum = forward_first(columns)
    row_index = lax.axis_index("rows")
    own_positions = row_index * row_count + jnp.arange(row_count, dtype=jnp.int32)
    freq_own = frequencies(own_positions)
    freq_whole = frequencies(jnp.arange(N, dtype=jnp.int32))
    spectrum = lax.all_to_all(
        jnp.swapaxes(spectrum, 1, 2), "rows", split_axis=2, concat_axis=1, tiled=True
    )
    depth_index = lax.axis_index("depth")
    distance = depth_start + depth_step * (depth_index * PL_DEV + 0).astype(jnp.float32)
    cosine_part, sine_part = propagator(freq_whole, freq_own, distance)
    propagated = propagate(spectrum, cosine_part, sine_part)
    propagated = lax.all_to_all(
        jnp.swapaxes(propagated, 1, 2), "rows", split_axis=2, concat_axis=1, tiled=True
    )
    halfway = inverse_first(propagated).astype(jnp.bfloat16)
    restored = lax.all_to_all(
        jnp.swapaxes(halfway, 1, 2), "rows", split_axis=2, concat_axis=1, tiled=True
    )
    result_field = inverse_first(restored)
    intensities = [
        (result_field[0] * result_field[0] + result_field[1] * result_field[1]).astype(jnp.bfloat16)
    ]
    stacked = jnp.stack(intensities)
    padded = padded_2(stacked, (("depth", 0), ("rows", 2)), 1)
    centre_block = padded[1:-1, :, 1:-1]
    plane_ids = jnp.arange(PL_DEV, dtype=jnp.int32)[:, None, None]
    row_ids = jnp.arange(row_count, dtype=jnp.int32)[None, None, :]
    depth_count = lax.axis_size("depth")
    row_groups = lax.axis_size("rows")
    lower_plane = jnp.where(
        (depth_index == 0) & (plane_ids == 0), centre_block, padded[:-2, :, 1:-1]
    )
    upper_plane = jnp.where(
        (depth_index == depth_count - 1) & (plane_ids == PL_DEV - 1),
        centre_block,
        padded[2:, :, 1:-1],
    )
    north_row = jnp.where((row_index == 0) & (row_ids == 0), centre_block, padded[1:-1, :, :-2])
    south_row = jnp.where(
        (row_index == row_groups - 1) & (row_ids == row_count - 1),
        centre_block,
        padded[1:-1, :, 2:],
    )
    centre = centre_block.astype(jnp.float32)
    east_col = jnp.concatenate([centre[:, 1:], centre[:, -1:]], axis=1)
    west_col = jnp.concatenate([centre[:, :1], centre[:, :-1]], axis=1)
    depth_diff = upper_plane.astype(jnp.float32) - lower_plane.astype(jnp.float32)
    row_diff = south_row.astype(jnp.float32) - north_row.astype(jnp.float32)
    col_diff = east_col - west_col
    scores = (depth_diff * depth_diff + row_diff * row_diff + col_diff * col_diff) / 8.0
    sharpest = jnp.max(scores, axis=0)
    merged = lax.pmax(sharpest.astype(jnp.bfloat16), "depth").astype(sharpest.dtype)
    return merged.T


def solution(mesh):
    in_specs = (P("rows", None), P("rows", None))
    out_specs = P("rows", None)
    return jax.shard_map(shards, mesh=mesh, in_specs=in_specs, out_specs=out_specs, check_vma=False)
```

profile of v0, /device:TPU:8, one launch (start us, length us, event | category | flops | bytes accessed | tf_op | source)
XLA Modules:
  0.0 712.9 jit_solution(13495898299766923649)
XLA Ops:
  7.0 1.6 copy.69
  10.7 1.4 subtract_convert_fusion.3
  12.3 1.7 fusion.32
  14.3 17.8 %copy.75 = bf16[2,128,4096]{1,0,2:T(2,128)(2,1)S(1)} copy(bf16[2,128,4096]{1,2,0:T(8,128)(2,1)S(1)} %bitcast.150) | data formatting | bytes 4194304 | tf_op jit(solution)/shard_map/transpose | solution.py:120
  32.1 57.8 %all_to_all.54 = bf16[2,128,4096]{1,0,2:T(2,128)(2,1)S(1)} all-to-all(bf16[2,128,4096]{1,0,2:T(2,128)(2,1)S(1)} %copy.75), channel_id=1, replica_groups=mesh['depth'=16,'rows'=32] {'rows'}, dimensions={2} | all-to-all | bytes 4194304 | tf_op jit(solution)/shard_map/all_to_all | solution.py:119
  89.9 1.6 copy.76
  91.5 3.1 copy.77
  94.7 1.7 convolution_bitcast_fusion.3
  96.3 1.4 subtract_convert_fusion.2
  97.9 1.7 fusion.35
  99.9 18.1 %copy.83 = bf16[2,128,4096]{1,0,2:T(2,128)(2,1)} copy(bf16[2,128,4096]{1,2,0:T(8,128)(2,1)S(1)} %bitcast.152) | data formatting | bytes 4194304 | tf_op jit(solution)/shard_map/transpose | solution.py:128
  118.0 6.1 all-to-all-start.1
  124.2 48.2 %all-to-all-done.1 = bf16[2,128,4096]{1,0,2:T(2,128)(2,1)S(1)} async-done(((bf16[2,128,4096]{1,0,2:T(2,128)(2,1)}), bf16[2,128,4096]{1,0,2:T(2,128)(2,1)S(1)}, u32[]{:S(2)}, u32[]{:S(2)}) %all-to-all-start.1) | async-done | bytes 2097184 | tf_op jit(solution)/shard_map/all_to_all | solution.py:127
  173.2 2.3 fusion.87
  175.5 1.9 copy.85
  177.4 2.9 copy.86
  180.3 12.3 %fusion.23 = (bf16[1,4096,128]{2,1,0:T(8,128)(2,1)S(1)}, bf16[1,4096,128]{2,1,0:T(8,128)(2,1)S(1)}) fusion(f32[1,32,128,128]{3,2,1,0:T(8,128)} %copy.86, f32[1,32,128,128]{3,2,1,0:T(8,128)S(1)} %copy.85, f32[]{:T(128)S(6)} %mul_shard_map.11, f32[128]{0:T(128)S(1)} %fusion.84, f32[4096]{0:T(1024)S(1)} %fusion.79, f32[]{:T(128)S(6)} %mul_shard_map.10), kind=kLoop, calls=%fused_computation.44 | loop fusion | flops 9437184 | bytes 6308360 | tf_op jit(solution)/shard_map/convert.7
  192.8 18.1 %copy.87 = bf16[2,128,4096]{1,0,2:T(2,128)(2,1)} copy(bf16[2,128,4096]{1,2,0:T(8,128)(2,1)S(1)} %maximum_bitcast_fusion.2) | data formatting | bytes 4194304 | tf_op jit(solution)/shard_map/transpose | solution.py:135
  211.0 6.3 all-to-all-start.2
  218.1 47.5 %all-to-all-done.2 = bf16[2,128,4096]{1,0,2:T(2,128)(2,1)S(1)} async-done(((bf16[2,128,4096]{1,0,2:T(2,128)(2,1)}), bf16[2,128,4096]{1,0,2:T(2,128)(2,1)S(1)}, u32[]{:S(2)}, u32[]{:S(2)}) %all-to-all-start.2) | async-done | bytes 2097184 | tf_op jit(solution)/shard_map/all_to_all | solution.py:134
  265.6 1.6 copy.88
  267.2 3.1 copy.89
  271.1 1.4 subtract_convert_fusion.1
  272.7 1.7 bitcast_convert_fusion
  274.4 1.4 copy.94
  275.8 18.1 %copy.95 = bf16[2,128,4096]{1,0,2:T(2,128)(2,1)} copy(bf16[2,128,4096]{1,2,0:T(8,128)(2,1)S(1)} %bitcast.154) | data formatting | bytes 4194304 | tf_op jit(solution)/shard_map/transpose | solution.py:139
  293.9 6.0 all-to-all-start.3
  300.2 48.0 %all-to-all-done.3 = bf16[2,128,4096]{1,0,2:T(2,128)(2,1)S(1)} async-done(((bf16[2,128,4096]{1,0,2:T(2,128)(2,1)}), bf16[2,128,4096]{1,0,2:T(2,128)(2,1)S(1)}, u32[]{:S(2)}, u32[]{:S(2)}) %all-to-all-start.3) | async-done | bytes 2097184 | tf_op jit(solution)/shard_map/all_to_all | solution.py:138
  348.3 1.6 copy.96
  349.9 3.1 copy.97
  353.8 1.4 subtract_convert_fusion
  355.4 1.7 convolution_bitcast_fusion
  358.2 1.3 collective-permute-start
  359.5 4.6 collective-permute-start.1
  364.4 2.3 fusion.89
  366.6 18.1 %collective-permute-done = bf16[1,4096,128]{2,1,0:T(8,128)(2,1)S(1)} collective-permute-done((bf16[1,4096,128]{2,1,0:T(8,128)(2,1)S(1)}, bf16[1,4096,128]{2,1,0:T(8,128)(2,1)S(1)}, u32[]{:S(2)}, u32[]{:S(2)}) %collective-permute-start) | collective-permute-done | bytes 1048608 | tf_op jit(solution)/shard_map/ppermute | solution.py:26
  384.7 1.2 collective-permute-done.1
  385.9 1.0 copy-done.2
  387.2 3.6 fusion.88
  390.9 3.5 copy.101
  394.3 1.9 collective-permute-start.2
  396.3 3.5 copy.103
  399.7 2.4 collective-permute-start.3
  402.2 2.9 copy.102
  405.1 2.9 copy.104
  408.0 5.9 fusion.43
  413.9 289.3 %all-reduce.2.cloned.1.call-done = bf16[128,4096]{0,1:T(8,128)(2,1)} async-done(((bf16[128,4096]{0,1:T(8,128)(2,1)}), bf16[128,4096]{0,1:T(8,128)(2,1)}) %all-reduce.2.cloned.1.call-update) | async-done | bytes 1048592 | tf_op jit(solution)/shard_map/pmax | solution.py:174
  703.3 2.6 copy.105
  (45 shorter events, 9.0 us)
Async XLA Ops:
  6.5 2.1 copy-start.3
  118.0 54.4 %all-to-all-start.1 = ((bf16[2,128,4096]{1,0,2:T(2,128)(2,1)}), bf16[2,128,4096]{1,0,2:T(2,128)(2,1)S(1)}, u32[]{:S(2)}, u32[]{:S(2)}) async-start(bf16[2,128,4096]{1,0,2:T(2,128)(2,1)} %copy.83), calls=%async_computation.1 | async-start | bytes 4194304 | tf_op jit(solution)/shard_map/all_to_all | solution.py:127
  211.0 54.6 %all-to-all-start.2 = ((bf16[2,128,4096]{1,0,2:T(2,128)(2,1)}), bf16[2,128,4096]{1,0,2:T(2,128)(2,1)S(1)}, u32[]{:S(2)}, u32[]{:S(2)}) async-start(bf16[2,128,4096]{1,0,2:T(2,128)(2,1)} %copy.87), calls=%async_computation.2 | async-start | bytes 4194304 | tf_op jit(solution)/shard_map/all_to_all | solution.py:134
  293.9 54.4 %all-to-all-start.3 = ((bf16[2,128,4096]{1,0,2:T(2,128)(2,1)}), bf16[2,128,4096]{1,0,2:T(2,128)(2,1)S(1)}, u32[]{:S(2)}, u32[]{:S(2)}) async-start(bf16[2,128,4096]{1,0,2:T(2,128)(2,1)} %copy.95), calls=%async_computation.3 | async-start | bytes 4194304 | tf_op jit(solution)/shard_map/all_to_all | solution.py:138
  299.9 403.4 %all-reduce.2.cloned.1.call-start = ((), (), s32[]{:S(2)}) async-start(), calls=%async_computation.4 | async-start | bytes 2097152 | tf_op jit(solution)/shard_map/pmax | solution.py:174
  358.2 26.5 %collective-permute-start = (bf16[1,4096,128]{2,1,0:T(8,128)(2,1)S(1)}, bf16[1,4096,128]{2,1,0:T(8,128)(2,1)S(1)}, u32[]{:S(2)}, u32[]{:S(2)}) collective-permute-start(bf16[1,4096,128]{2,1,0:T(8,128)(2,1)S(1)} %bitcast.142), channel_id=1, source_target_pairs={{32,0},{64,32},{96,64},{128,96},{160,128},{192,160},{224,192},{256... | collective-permute-start | bytes 3145736 | tf_op jit(solution)/shard_map/ppermute | solution.py:26
  359.5 26.4 %collective-permute-start.1 = (bf16[1,4096,128]{2,1,0:T(8,128)(2,1)S(1)}, bf16[1,4096,128]{2,1,0:T(8,128)(2,1)S(1)}, u32[]{:S(2)}, u32[]{:S(2)}) collective-permute-start(bf16[1,4096,128]{2,1,0:T(8,128)(2,1)S(1)} %bitcast.143), channel_id=1, source_target_pairs={{0,32},{32,64},{64,96},{96,128},{128,160},{160,192},{192,224},{224... | collective-permute-start | bytes 3145736 | tf_op jit(solution)/shard_map/ppermute | solution.py:23
  384.7 1.2 copy-start.1
  385.9 1.0 copy-start.2
  394.3 7.8 %collective-permute-start.2 = (bf16[3,4096,1]{1,0,2:T(4,128)(2,1)S(1)}, bf16[3,4096,1]{1,0,2:T(4,128)(2,1)S(1)}, u32[]{:S(2)}, u32[]{:S(2)}) collective-permute-start(bf16[3,4096,1]{1,0,2:T(4,128)(2,1)S(1)} %copy.101), channel_id=1, source_target_pairs={{1,0},{2,1},{3,2},{4,3},{5,4},{6,5},{7,6},{8,7},{9,8},{10,9},{11,1... | collective-permute-start | bytes 73736 | tf_op jit(solution)/shard_map/ppermute | solution.py:26
  399.7 5.4 collective-permute-start.3
  405.1 2.9 copy-start
Sparse Core Ops, SparseCore 0:
  414.1 289.1 all-reduce.1
where the time goes:
time: 718 us; the launch traced here: 713 us
  waiting for transfers between devices  452 us (63%)
  local copies, waits for them, and re-layouts  121 us (17%)
  blocking collectives  57.8 us (8%)
  starting transfers between devices  29 us (4%)
  other arithmetic  27.9 us (4%)
  between operations  14.1 us (2%)
  matrix products  11 us (2%)
    pmax x1, waiting for transfers between devices, shards(): lax.pmax(sharpest.astype(jnp.bfloat16), 'depth').astype(sharpest.dtype)  289 us
    all_to_all x1, blocking collectives, shards(): lax.all_to_all(jnp.swapaxes(along_rows, 1, 2), 'rows', split_axis=2, conc...  57.8 us
    all_to_all x1, waiting for transfers between devices, shards(): lax.all_to_all(jnp.swapaxes(spectrum, 1, 2), 'rows', split_axis=2, concat...  48.2 us
    all_to_all x1, waiting for transfers between devices, shards(): lax.all_to_all(jnp.swapaxes(halfway, 1, 2), 'rows', split_axis=2, concat_...  48 us
    all_to_all x1, waiting for transfers between devices, shards(): lax.all_to_all(jnp.swapaxes(propagated, 1, 2), 'rows', split_axis=2, conc...  47.5 us
    another operation x9, other arithmetic  18.5 us
    transpose x1, local copies, waits for them, and re-layouts, shards(): jnp.swapaxes(propagated, 1, 2)  18.1 us
    transpose x1, local copies, waits for them, and re-layouts, shards(): jnp.swapaxes(halfway, 1, 2)  18.1 us
  transfers between devices with their start and end apart: 8, of which 6 were waited for; matrix products, arithmetic and copies ran while one was open for 1% of the time, Pallas kernels for 0%

commit v1 on v0

v1 whole, which is shorter than its diff:
```python
import functools
import math

import jax
import jax.numpy as jnp
from jax import lax
from jax.experimental import pallas as pl
from jax.experimental.pallas import tpu as pltpu
from jax.sharding import Mesh
from jax.sharding import PartitionSpec as P

N = 4096
RADIX = 64
PLANES = 16
AXES = ("zh", "x", "zl", "y", "c")
SIZES = (4, 4, 4, 4, 2)
MESH = pl.DeviceIdType.MESH

wave_number = 0.6
depth_start = 8.0
depth_step = 2.0


def fourier_tables(radix_size, sign_value):
    indices = jnp.arange(radix_size, dtype=jnp.int32)
    products = indices[:, None] * indices[None, :] % radix_size
    angles = products.astype(jnp.float32) * (sign_value * 2.0 * math.pi / radix_size)
    scaling = 1.0 / math.sqrt(radix_size)
    cosine_part = jnp.cos(angles) * scaling
    sine_part = jnp.sin(angles) * scaling
    matrix = jnp.stack([jnp.stack([cosine_part, -sine_part]), jnp.stack([sine_part, cosine_part])])
    return matrix.astype(jnp.bfloat16)


def twiddle_table(radix_size, sign_value):
    indices = jnp.arange(radix_size, dtype=jnp.int32)
    total = radix_size * radix_size
    products = indices[:, None] * indices[None, :] % total
    angles = products.astype(jnp.float32) * (sign_value * 2.0 * math.pi / total)
    return (jnp.cos(angles), jnp.sin(angles))


def rotate(data, cosine_part, sine_part):
    return jnp.stack(
        [data[0] * cosine_part - data[1] * sine_part, data[0] * sine_part + data[1] * cosine_part]
    )


def contract(form, matrix, data):
    return jnp.einsum(form, matrix, data, preferred_element_type=jnp.float32)


def forward_first(data):
    batch_size = data.shape[2]
    shaped = data.reshape(2, RADIX, RADIX, batch_size)
    matrix = fourier_tables(RADIX, -1.0)
    cosine_part, sine_part = twiddle_table(RADIX, -1.0)
    opening = contract("ocka,cabm->okbm", matrix, shaped)
    sectioned = rotate(opening, cosine_part[:, :, None], sine_part[:, :, None]).astype(jnp.bfloat16)
    closing = contract("ocjb,ckbm->okjm", matrix, sectioned)
    return closing.reshape(2, N, batch_size).astype(jnp.bfloat16)


def inverse_first(data):
    batch_size = data.shape[2]
    shaped = data.reshape(2, RADIX, RADIX, batch_size)
    matrix = fourier_tables(RADIX, 1.0)
    cosine_part, sine_part = twiddle_table(RADIX, 1.0)
    opening = contract("ocbj,ckjm->okbm", matrix, shaped)
    sectioned = rotate(opening, cosine_part[:, :, None], sine_part[:, :, None]).astype(jnp.bfloat16)
    closing = contract("ocak,ckbm->oabm", matrix, sectioned)
    return closing.reshape(2, N, batch_size)


def row_sections(contrast, first):
    batch_size = contrast.shape[0]
    shaped = contrast.T.reshape(RADIX, RADIX, batch_size)
    matrix = fourier_tables(RADIX, -1.0)
    cosine_part, sine_part = twiddle_table(RADIX, -1.0)
    part = functools.partial(lax.dynamic_slice_in_dim, start_index=first, slice_size=16)
    opening = contract("oka,abm->okbm", part(matrix[:, 0], axis=1), shaped)
    cosine_part, sine_part = part(cosine_part, axis=0), part(sine_part, axis=0)
    sectioned = rotate(opening, cosine_part[:, :, None], sine_part[:, :, None]).astype(jnp.bfloat16)
    closing = contract("ocjb,ckbm->komj", matrix, sectioned).astype(jnp.bfloat16)
    paired = closing.reshape(8, 2, 2, batch_size, RADIX)
    return paired.transpose(0, 2, 3, 1, 4).reshape(8, 2, batch_size, 2 * RADIX)


def place():
    return {name: lax.axis_index(name) for name in AXES}


def remote(source, target, send_sem, recv_sem, device):
    return pltpu.make_async_remote_copy(
        src_ref=source,
        dst_ref=target,
        send_sem=send_sem,
        recv_sem=recv_sem,
        device_id=device,
        device_id_type=MESH,
    )


def greet(sources, count):
    barrier = pltpu.get_barrier_semaphore()
    for device in sources:
        pl.semaphore_signal(barrier, inc=1, device_id=device, device_id_type=MESH)
    pl.semaphore_wait(barrier, count)


def call(kernel, name, number, out_shapes, scratch, args, vmem=None):
    params = {"vmem_limit_bytes": vmem} if vmem else {}
    if number is not None:
        params |= {"collective_id": number, "has_side_effects": True}
    return pl.pallas_call(
        kernel,
        name=name,
        out_shape=out_shapes,
        in_specs=[pl.BlockSpec(memory_space=pltpu.VMEM)] * len(args),
        out_specs=jax.tree.map(lambda _: pl.BlockSpec(memory_space=pltpu.VMEM), out_shapes),
        scratch_shapes=scratch,
        compiler_params=pltpu.CompilerParams(**params),
    )(*args)


def propagate_kernel(sections, columns, k_real, k_imag, send_sem, recv_sem, own_sem):
    at = place()
    x, yc, z = at["x"], at["y"] * 2 + at["c"], at["zh"] * 4 + at["zl"]
    slab = at["zl"] * 8 + yc

    def device(step, turn):
        to, layer = lax.rem(yc + step + 8, 8), lax.rem(z + turn + 16, 16)
        return {
            "zh": layer // 4,
            "x": x,
            "zl": lax.rem(layer, 4),
            "y": to // 2,
            "c": lax.rem(to, 2),
        }

    moves = []
    for turn in (2, 1, -1, 0):
        for step in range(8):
            if (step, turn) != (0, 0):
                moves.append((step, -2 if turn == 2 and step >= 4 else turn))
    greet([device(-step, -turn) for step, turn in moves], len(moves))
    mine = columns.at[:, pl.ds(slab * 128, 128), :]
    copies = []
    for index, (step, turn) in enumerate(moves):
        copies.append(
            remote(
                sections.at[lax.rem(yc + step, 8)],
                mine,
                send_sem.at[index],
                recv_sem.at[slab],
                device(step, turn),
            )
        )
        copies[-1].start()
    own = pltpu.make_async_copy(sections.at[yc], mine, own_sem)
    own.start()

    distance = depth_start + depth_step * z.astype(jnp.float32)
    lane = lax.broadcasted_iota(jnp.int32, (RADIX, 128), 1)
    row = lax.broadcasted_iota(jnp.int32, (RADIX, 128), 0)
    ring = (x * 8 + yc) * 2 + lane // RADIX + RADIX * lax.rem(lane, RADIX)
    ring = jnp.where(ring >= N // 2, ring - N, ring).astype(jnp.float32) / N
    column_part = ring * ring
    base = RADIX * row
    base = jnp.where(base >= N // 2, base - N, base)
    limit = wave_number * wave_number

    def tile(k, carry):
        freq = (base + k).astype(jnp.float32) / N
        radial = freq * freq + column_part
        amplitude = jnp.exp(
            (-2.0 * math.pi * distance) * jnp.sqrt(jnp.maximum(radial - limit, 0.0))
        )
        turns = distance * (jnp.sqrt(jnp.maximum(limit - radial, 0.0)) - wave_number)
        half = (turns - jnp.floor(turns + 0.5)) * math.pi
        square = half * half
        sine, cosine = jnp.full_like(half, 0.0), jnp.full_like(half, 0.0)
        for power in range(6, -1, -1):
            cosine = cosine * square + (-1) ** power / math.factorial(2 * power)
            if power < 6:
                sine = sine * square + (-1) ** power / math.factorial(2 * power + 1)
        sine = sine * half
        k_real[pl.ds(k * RADIX, RADIX), :] = amplitude * (1.0 - 2.0 * sine * sine)
        k_imag[pl.ds(k * RADIX, RADIX), :] = amplitude * (2.0 * sine * cosine)
        return carry

    lax.fori_loop(0, RADIX, tile, 0)

    own.wait()
    for copy in copies:
        copy.wait_send()
    for step, turn in moves:
        origin = lax.rem(lax.rem(z - turn + 16, 16), 4) * 8 + lax.rem(yc - step + 8, 8)
        slot = columns.at[:, pl.ds(origin * 128, 128), :]
        remote(slot, slot, own_sem, recv_sem.at[origin], device(-step, -turn)).wait_recv()


def layer_kernel(halfway, gathered, send_sem, recv_sem, own_sem):
    at = place()
    me = at["x"] * 8 + at["y"] * 2 + at["c"]

    def device(other):
        return {
            "zh": at["zh"],
            "x": other // 8,
            "zl": at["zl"],
            "y": lax.rem(other // 2, 4),
            "c": lax.rem(other, 2),
        }

    others = [lax.rem(me + step, 32) for step in range(1, 32)]
    greet([device(other) for other in others], 31)
    copies = []
    for other in others:
        copies.append(
            remote(
                halfway.at[:, :, lax.rem(other, 8), other // 8],
                gathered.at[me],
                send_sem.at[other],
                recv_sem.at[me],
                device(other),
            )
        )
        copies[-1].start()
    own = pltpu.make_async_copy(
        halfway.at[:, :, lax.rem(me, 8), me // 8], gathered.at[me], own_sem
    )
    own.start()
    own.wait()
    for copy in copies:
        copy.wait_send()
    for other in others:
        slot = gathered.at[other]
        remote(slot, slot, own_sem, recv_sem.at[other], device(other)).wait_recv()


def inverse_rows_kernel(gathered, first, second, cosines, sines, eye, out, middle, turned):
    def opening(s, carry):
        data = jnp.concatenate([gathered[s, 0], gathered[s, 1]], axis=1)
        made = lax.dot_general(
            first[...], data, (((1,), (1,)), ((), ())), preferred_element_type=jnp.float32
        )
        real, imag = made[:128], made[128:]
        cosine_part, sine_part = cosines[s], sines[s]
        parts = (
            real * cosine_part - imag * sine_part,
            real * sine_part + imag * cosine_part,
        )
        for which, part in enumerate(parts):
            for half in range(2):
                middle[pl.ds(which * RADIX + 2 * s + half, RADIX, stride=128), :] = part[
                    half * RADIX : (half + 1) * RADIX
                ]
        return carry

    lax.fori_loop(0, 32, opening, 0)

    def closing(b, carry):
        block = middle[pl.ds(b * 128, 128), :].astype(jnp.bfloat16)
        made = jnp.dot(second[...], block, preferred_element_type=jnp.float32)
        real, imag = made[:RADIX], made[RADIX:]
        turned[pl.ds(b, RADIX, stride=RADIX), :] = real * real + imag * imag
        return carry

    lax.fori_loop(0, RADIX, closing, 0)

    for t in range(32):
        block = turned[t * 128 : (t + 1) * 128, :].astype(jnp.bfloat16)
        made = lax.dot_general(
            eye[...], block, (((1,), (1,)), ((), ())), preferred_element_type=jnp.float32
        )
        out[:, :, t * 128 : (t + 1) * 128] = made.reshape(16, 8, 128).astype(jnp.bfloat16)


def depth_kernel(planes, stack, send_sem, recv_sem, own_sem):
    at = place()
    z = at["zh"] * 4 + at["zl"]

    def device(layer):
        return {**at, "zh": layer // 4, "zl": lax.rem(layer, 4)}

    def piece(layer):
        return planes.at[lax.rem(layer, 4) * 4 + layer // 4]

    others = [lax.rem(z + step, 16) for step in (8, 7, 9, 6, 10, 5, 11, 4, 12, 3, 13, 2, 14, 1, 15)]
    greet([device(other) for other in others], 15)
    copies = []
    for other in others:
        copies.append(
            remote(
                piece(other), stack.at[z], send_sem.at[other], recv_sem.at[z], device(other)
            )
        )
        copies[-1].start()
    own = pltpu.make_async_copy(piece(z), stack.at[z], own_sem)
    own.start()
    own.wait()
    for copy in copies:
        copy.wait_send()
    for other in others:
        slot = stack.at[other]
        remote(slot, slot, own_sem, recv_sem.at[other], device(other)).wait_recv()


def edge_kernel(low, high, north, south, send_sem, recv_sem):
    at = place()
    q = (((at["zl"] * 4 + at["y"]) * 2 + at["c"]) * 4 + at["x"]) * 4 + at["zh"]

    def device(other):
        return {
            "zh": lax.rem(other, 4),
            "x": lax.rem(other // 4, 4),
            "zl": other // 128,
            "y": lax.rem(other // 32, 4),
            "c": lax.rem(other // 16, 2),
        }

    ahead, behind = device(lax.rem(q + 1, 512)), device(lax.rem(q + 511, 512))
    greet([ahead, behind], 2)
    copies = [
        remote(high, north, send_sem.at[0], recv_sem.at[0], ahead),
        remote(low, south, send_sem.at[1], recv_sem.at[1], behind),
    ]
    for copy in copies:
        copy.start()
    for copy in copies:
        copy.wait()


def spread_kernel(piece, out, send_sem, recv_sem, own_sem):
    at = place()
    x, zh = at["x"], at["zh"]

    def across(step):
        return {**at, "x": lax.rem(x + step + 4, 4)}

    def along(step):
        return {**at, "zh": lax.rem(zh + step + 4, 4)}

    greet([across(s) for s in (1, 2, 3)] + [along(s) for s in (1, 2, 3)], 6)
    copies = []

    def send(source, level, device):
        copies.append(
            remote(
                source,
                out.at[x, level],
                send_sem.at[len(copies)],
                recv_sem.at[x, level],
                device,
            )
        )
        copies[-1].start()

    for step in (2, 1, 3):
        send(piece, zh, along(step))
    for step in (2, 1, 3):
        send(piece, zh, across(step))
    own = pltpu.make_async_copy(piece, out.at[x, zh], own_sem)
    own.start()
    for step in (1, 3, 2):
        level = lax.rem(zh + step, 4)
        slot = out.at[x, level]
        remote(slot, slot, own_sem, recv_sem.at[x, level], along(step)).wait_recv()
        for turn in (2, 1, 3):
            send(slot, level, across(turn))
    own.wait()
    for step in (1, 2, 3):
        for level in range(4):
            slot = out.at[lax.rem(x + step, 4), level]
            remote(
                slot, slot, own_sem, recv_sem.at[lax.rem(x + step, 4), level], across(step)
            ).wait_recv()
    for copy in copies:
        copy.wait_send()


def scores_of(stack, north, south):
    centre = stack.astype(jnp.float32)
    lower = jnp.concatenate([centre[:1], centre[:-1]], axis=0)
    upper = jnp.concatenate([centre[1:], centre[-1:]], axis=0)
    above = jnp.concatenate([north[:, None].astype(jnp.float32), centre[:, :-1]], axis=1)
    below = jnp.concatenate([centre[:, 1:], south[:, None].astype(jnp.float32)], axis=1)
    east = jnp.concatenate([centre[..., 1:], centre[..., -1:]], axis=-1)
    west = jnp.concatenate([centre[..., :1], centre[..., :-1]], axis=-1)
    depth_diff, row_diff, col_diff = upper - lower, below - above, east - west
    scores = (depth_diff * depth_diff + row_diff * row_diff + col_diff * col_diff) / 8.0
    return jnp.max(scores, axis=0)


def inverse_row_tables():
    matrix = fourier_tables(RADIX, 1.0)
    pair = jnp.eye(2, dtype=jnp.bfloat16)
    first = jnp.einsum("ocbj,kl->okbclj", matrix, pair).reshape(256, 256)
    second = jnp.einsum("ocak->oack", matrix).reshape(128, 128)
    cosine_part, sine_part = twiddle_table(RADIX, 1.0)
    wide = lambda part: jnp.broadcast_to(part.reshape(32, 128, 1), (32, 128, 128))
    return first, second, wide(cosine_part), wide(sine_part), jnp.eye(128, dtype=jnp.bfloat16)


def shards(hologram, background):
    at = place()
    bf16, f32 = jnp.bfloat16, jnp.float32
    shape = jax.ShapeDtypeStruct
    dma = pltpu.SemaphoreType.DMA
    contrast = (hologram.astype(f32) / background.astype(f32) - 1.0).astype(bf16)
    sections = row_sections(contrast, at["x"] * 16)
    columns, k_real, k_imag = call(
        propagate_kernel,
        "columns",
        0,
        (shape((2, N, 128), bf16), shape((N, 128), f32), shape((N, 128), f32)),
        [dma((31,)), dma((32,)), dma],
        (sections,),
    )
    spectrum = forward_first(columns)
    propagated = rotate(spectrum.astype(f32), k_real, k_imag).astype(bf16)
    halfway = inverse_first(propagated).astype(bf16)
    gathered = call(
        layer_kernel,
        "layer",
        1,
        shape((32, 2, 4, 32, 128), bf16),
        [dma((32,)), dma((32,)), dma],
        (halfway.reshape(2, 4, 8, 4, 32, 128),),
    )
    planes = call(
        inverse_rows_kernel,
        "rows",
        None,
        shape((16, 8, N), bf16),
        [pltpu.VMEM((RADIX * 128, 128), f32), pltpu.VMEM((N, 128), f32)],
        (gathered.reshape(32, 2, 128, 128), *inverse_row_tables()),
        48 << 20,
    )
    stack = call(
        depth_kernel,
        "depth",
        2,
        shape((PLANES, 8, N), bf16),
        [dma((16,)), dma((16,)), dma],
        (planes,),
    )
    north, south = call(
        edge_kernel,
        "edges",
        3,
        (shape((PLANES, N), bf16), shape((PLANES, N), bf16)),
        [dma((2,)), dma((2,))],
        (stack[:, 0], stack[:, 7]),
    )
    q = (((at["zl"] * 4 + at["y"]) * 2 + at["c"]) * 4 + at["x"]) * 4 + at["zh"]
    north = jnp.where(q == 0, stack[:, 0], north)
    south = jnp.where(q == 511, stack[:, 7], south)
    sharpest = scores_of(stack, north, south).astype(bf16)
    merged = call(
        spread_kernel,
        "spread",
        4,
        shape((4, 4, 8, N), bf16),
        [dma((15,)), dma((4, 4)), dma],
        (sharpest,),
    )
    return merged.reshape(128, N).astype(f32)


def solution(mesh):
    fine = Mesh(mesh.devices.reshape(SIZES), AXES)
    spec = P(("zl", "y", "c"), None)
    return jax.shard_map(
        shards, mesh=fine, in_specs=(spec, spec), out_specs=spec, check_vma=False
    )
```

time: 718 us -> 271 us (0.38)
  the two profiles are of different devices: /device:TPU:8 before, /device:TPU:120 now
where the time goes in v1:
time: 271 us
  Pallas kernels  225 us (83%)
  local copies, waits for them, and re-layouts  18.5 us (7%)
  other arithmetic  16.4 us (6%)
  matrix products  10.4 us (4%)
    pallas_call x6, Pallas kernels, call(): pl.pallas_call(kernel, name=name, out_shape=out_shapes, in_specs=[pl.Bloc...  225 us
    dot_general x6, matrix products, contract(): return jnp.einsum(form, matrix, data, preferred_element_type=jnp.float32)  10.4 us
    another operation x10, other arithmetic  6.82 us
    unnamed x16, local copies, waits for them, and re-layouts  6.76 us

profile of v1, /device:TPU:120, one launch (start us, length us, event | category | flops | bytes accessed | tf_op | source)
XLA Modules:
  0.0 270.9 jit_solution(14222360416150970169)
XLA Ops:
  0.0 0.1 fusion.42
  0.3 0.1 negate_convert_fusion
  0.5 1.6 copy.20
  2.1 0.7 copy.21
  2.8 0.4 add_convert_fusion.2
  3.2 0.8 fusion.21
  4.4 0.3 subtract_convert_fusion.2
  4.8 0.3 fusion.20
  5.2 1.0 copy.25.sections
  6.2 38.9 %columns.1 = (bf16[2,4096,128]{2,1,0:T(8,128)(2,1)}, f32[4096,128]{1,0:T(8,128)}, f32[4096,128]{1,0:T(8,128)}) custom-call(bf16[8,2,128,128]{3,2,1,0:T(8,128)(2,1)} %copy.25.sections), custom_call_target="tpu_custom_call" | custom-call | tf_op jit(solution)/shard_map/columns/pallas_call | solution.py:115
  45.1 3.2 %convolution_bitcast_fusion.1 = f32[2,64,64,128]{3,1,2,0:T(8,128)S(1)} fusion(bf16[2,64,64,128]{3,2,1,0:T(8,128)(2,1)} %bitcast.137, bf16[1,2,64,64]{3,2,1,0:T(8,128)(2,1)S(1)} %get-tuple-element.44, bf16[1,2,64,64]{3,2,1,0:T(8,128)(2,1)S(1)} %get-tuple-element.43), kind=kOutput, calls=%fused_computation.4 | convolution fusion | flops 268500992 | bytes 6324224 | tf_op jit(solution)/shard_map/ocka,cabm->okbm/dot_general | solution.py:50
  48.3 1.4 subtract_convert_fusion.1
  49.7 0.2 maximum_bitcast_fusion
  49.9 1.6 convert_bitcast_fusion
  51.6 0.3 fusion.57
  51.9 1.3 copy-done.3
  53.2 0.6 copy-done.4
  53.8 0.5 fusion.11
  54.4 0.2 negate_convert_fusion.1
  54.5 0.1 fusion.41
  54.7 2.7 convolution_bitcast_fusion
  57.6 0.2 multiply_sine_fusion
  57.8 3.8 %subtract_convert_fusion = (bf16[1,64,64,128]{3,2,0,1:T(8,128)(2,1)S(1)}, bf16[1,64,64,128]{3,2,0,1:T(8,128)(2,1)S(1)}) fusion(f32[2,64,64,128]{3,2,0,1:T(8,128)} %convolution_bitcast_fusion, f32[64,64]{1,0:T(8,128)S(1)} %copy.31, f32[64,64]{1,0:T(8,128)S(1)} %copy.30), kind=kLoop, calls=%fused_computation.34 | loop fusion | flops 4194304 | bytes 6324224 | tf_op jit(solution)/shard_map/convert.5
  61.6 0.2 pad_maximum_fusion
  61.9 1.7 bitcast_convert_fusion
  63.6 2.7 copy.33
  66.3 46.1 %layer.1 = bf16[32,2,4,32,128]{4,3,2,1,0:T(8,128)(2,1)} custom-call(bf16[2,4,8,4,32,128]{5,4,3,2,1,0:T(8,128)(2,1)} %bitcast.133), custom_call_target="tpu_custom_call" | custom-call | tf_op jit(solution)/shard_map/layer/pallas_call | solution.py:115
  112.5 0.3 multiply_bitcast_fusion
  112.8 0.2 reshape.285.first
  113.6 0.6 broadcast_in_dim.4.cosines
  114.2 1.9 broadcast_in_dim.5.sines
  116.1 22.4 %rows.1.planes = bf16[16,8,4096]{2,1,0:T(8,128)(2,1)S(1)} custom-call(bf16[32,2,128,128]{3,2,1,0:T(8,128)(2,1)S(1)} %bitcast.132, bf16[256,256]{1,0:T(8,128)(2,1)S(1)} %reshape.285.first, bf16[128,128]{1,0:T(8,128)(2,1)S(1)} %reshape.286.second, f32[32,128,128]{2,1,0:T(8,128)S(1)} %broadcast_in_dim.4.cosines, f32[32,128,128]{2,1,0:T(8,128)} %broadcast_in_dim.5.sines, ...), custom_call_target="tpu_custom_call" | custom-call | tf_op jit(solution)/shard_map/rows/pallas_call | solution.py:115
  138.5 1.0 copy-done.1
  139.5 59.4 %depth.1 = bf16[16,8,4096]{2,1,0:T(8,128)(2,1)} custom-call(bf16[16,8,4096]{2,1,0:T(8,128)(2,1)} %copy-done.1), custom_call_target="tpu_custom_call" | custom-call | tf_op jit(solution)/shard_map/depth/pallas_call | solution.py:115
  198.9 2.2 fusion.61
  201.1 0.8 copy.81
  201.9 0.8 copy.82
  202.7 20.9 %edges.1 = (bf16[16,4096]{1,0:T(8,128)(2,1)}, bf16[16,4096]{1,0:T(8,128)(2,1)}) custom-call(bf16[16,4096]{1,0:T(8,128)(2,1)} %bitcast.140, bf16[16,4096]{1,0:T(8,128)(2,1)} %bitcast.141), custom_call_target="tpu_custom_call" | custom-call | tf_op jit(solution)/shard_map/edges/pallas_call | solution.py:115
  223.6 1.1 bitcast_convert_fusion.3
  224.7 0.3 copy.39
  225.0 1.1 bitcast_convert_fusion.4
  226.0 0.3 copy.38
  226.3 0.5 fusion.59
  226.8 0.4 fusion.60
  227.3 0.4 fusion.63
  227.8 2.8 %fusion.6.piece = bf16[8,4096]{1,0:T(8,128)(2,1)} fusion(f32[1,8,4096]{2,1,0:T(8,128)S(1)} %get-tuple-element.34, f32[15,8,4096]{2,1,0:T(8,128)S(1)} %get-tuple-element.36, f32[15,8,4096]{2,1,0:T(8,128)S(1)} %get-tuple-element.35, f32[1,8,4096]{2,1,0:T(8,128)S(1)} %get-tuple-element.33, f32[16,1,4096]{2,1,0:T(1,128)S(1)} %copy.38, ...), kind=kLoop, calls=%fused_computation.15 | loop fusion | flops 8355840 | bytes 12648448 | tf_op jit(solution)/shard_map/reduce_max | solution.py:393
  230.6 37.5 %spread.1 = bf16[4,4,8,4096]{3,2,1,0:T(8,128)(2,1)} custom-call(bf16[8,4096]{1,0:T(8,128)(2,1)} %fusion.6.piece), custom_call_target="tpu_custom_call" | custom-call | tf_op jit(solution)/shard_map/spread/pallas_call | solution.py:115
  268.1 2.8 %bitcast_convert_fusion.2 = f32[128,4096]{1,0:T(8,128)} fusion(bf16[4,4,8,4096]{3,2,1,0:T(8,128)(2,1)} %spread.1), kind=kLoop, calls=%fused_computation.40 | loop fusion | flops 524288 | bytes 3145728 | tf_op jit(solution)/shard_map/convert_element_type | solution.py:469
  (35 shorter events, 1.7 us)
Async XLA Ops:
  0.0 2.1 copy-start.5
  51.6 1.6 copy-start.3
  51.6 2.2 copy-start.4
  113.6 2.6 copy-start
  138.5 1.0 copy-start.1
  198.9 27.5 %copy-start.2 = (bf16[16,8,4096]{2,1,0:T(8,128)(2,1)S(1)}, bf16[16,8,4096]{2,1,0:T(8,128)(2,1)}, u32[]{:S(2)}) copy-start(bf16[16,8,4096]{2,1,0:T(8,128)(2,1)} %depth.1) | copy-start | bytes 3145732

commit v2 on v0

v2 whole, which is shorter than its diff:
```python
import functools
import math

import jax
import jax.numpy as jnp
import numpy as np
from jax import lax
from jax.experimental import pallas as pl
from jax.experimental.pallas import tpu as pltpu
from jax.sharding import Mesh
from jax.sharding import PartitionSpec as P

N = 4096
RADIX = 64
PLANES = 16
AXES = ("zh", "x", "zl", "y", "c")
SIZES = (4, 4, 4, 4, 2)
MESH = pl.DeviceIdType.MESH
NT = (((1,), (1,)), ((), ()))
F32 = jnp.float32
BF16 = jnp.bfloat16

wave_number = 0.6
depth_start = 8.0
depth_step = 2.0


def fourier_tables(sign_value):
    indices = np.arange(RADIX)
    angles = (indices[:, None] * indices[None, :] % RADIX) * (sign_value * 2.0 * math.pi / RADIX)
    real, imag = np.cos(angles) / math.sqrt(RADIX), np.sin(angles) / math.sqrt(RADIX)
    matrix = np.stack([np.stack([real, -imag]), np.stack([imag, real])])
    return matrix.astype(np.float32)


def twiddle_table(sign_value):
    indices = np.arange(RADIX)
    angles = (indices[:, None] * indices[None, :]) * (sign_value * 2.0 * math.pi / N)
    return np.cos(angles).astype(np.float32), np.sin(angles).astype(np.float32)


def pass_tables():
    ahead, back = fourier_tables(-1.0), fourier_tables(1.0)
    flat = lambda table: table.transpose(0, 2, 1, 3).reshape(128, 128)
    both = np.zeros((2, 2, 2, RADIX, 2, 128), np.float32)
    for lane in range(128):
        far, j = divmod(lane, RADIX)
        both[1, :, far, :, :, lane] = back[:, :, :, RADIX - 1 - j if far else j].transpose(0, 2, 1)
        if j >= RADIX // 2:
            half, j = 1, (95 - j if far else j - 32)
        else:
            half, j = 0, ((RADIX - j if j else 32) if far else j)
        both[0, :, half, :, :, lane] = back[:, :, :, j].transpose(0, 2, 1)
    tables = (
        ahead[:, 0].reshape(128, RADIX),
        flat(ahead),
        flat(back),
        both.reshape(2, 256, 256),
        np.eye(128, dtype=np.float32),
    )
    return [jnp.asarray(table, BF16) for table in tables]


def row_sections(contrast, x):
    batch_size = contrast.shape[0]
    shaped = contrast.T.reshape(RADIX, RADIX, batch_size)
    matrix = jnp.asarray(fourier_tables(-1.0), BF16)
    cosine_part, sine_part = (jnp.asarray(part) for part in twiddle_table(-1.0))

    def part(table, axis):
        own = lax.dynamic_slice_in_dim(table, x * 8, 8, axis=axis)
        return jnp.concatenate([own, lax.slice_in_dim(table, 32, 33, axis=axis)], axis=axis)

    contract = functools.partial(jnp.einsum, preferred_element_type=F32)
    opening = contract("oka,abm->okbm", part(matrix[:, 0], 1), shaped)
    cosine_part, sine_part = part(cosine_part, 0)[:, :, None], part(sine_part, 0)[:, :, None]
    sectioned = jnp.stack(
        [
            opening[0] * cosine_part - opening[1] * sine_part,
            opening[0] * sine_part + opening[1] * cosine_part,
        ]
    ).astype(BF16)
    closing = contract("ocjb,ckbm->kmoj", matrix, sectioned).astype(BF16)
    zero, middle = closing[0], closing[8]
    packed = jnp.concatenate(
        [
            jnp.stack([zero[:, 0, :1], zero[:, 0, 32:33]], axis=1),
            zero[:, :, 1:32],
            middle[:, :, :32],
        ],
        axis=2,
    )
    chosen = jnp.where(x == 0, packed, zero)
    return jnp.concatenate([chosen[None], closing[1:8]]).reshape(8, batch_size, 128)


def remote(source, target, send_sem, recv_sem, device):
    return pltpu.make_async_remote_copy(
        src_ref=source,
        dst_ref=target,
        send_sem=send_sem,
        recv_sem=recv_sem,
        device_id=device,
        device_id_type=MESH,
    )


def sine_cosine(turns):
    half = (turns - jnp.floor(turns + 0.5)) * math.pi
    square = half * half
    sine, cosine = jnp.zeros_like(half), jnp.zeros_like(half)
    for power in range(6, -1, -1):
        cosine = cosine * square + (-1) ** power / math.factorial(2 * power)
        if power < 6:
            sine = sine * square + (-1) ** power / math.factorial(2 * power + 1)
    sine = sine * half
    return 2.0 * sine * cosine, 1.0 - 2.0 * sine * sine


def make_tables(me, z, cosines, sines, k_real, k_imag):
    distance = depth_start + depth_step * z.astype(F32)
    lane = lax.broadcasted_iota(jnp.int32, (RADIX, 128), 1)
    row = lax.broadcasted_iota(jnp.int32, (RADIX, 128), 0)
    j = lax.rem(lane, RADIX)
    general = me + RADIX * j
    lone = jnp.where(j == 0, jnp.where(lane >= RADIX, N // 2, 0), RADIX * j)
    lone = jnp.where(j >= RADIX // 2, 32 + RADIX * (j - RADIX // 2), lone)
    natural = jnp.where(me == 0, lone, general)
    freq = jnp.where(natural >= N // 2, natural - N, natural).astype(F32) / N
    column_part = freq * freq
    base = jnp.where(row >= RADIX // 2, RADIX * row - N, RADIX * row)
    limit = wave_number * wave_number

    def tile(k, carry):
        here = pl.ds(k * RADIX, RADIX)
        sine, cosine = sine_cosine((row * k).astype(F32) / N)
        cosines[k], sines[k] = cosine, sine
        freq = (base + k).astype(F32) / N
        radial = freq * freq + column_part
        amplitude = jnp.exp(
            (-2.0 * math.pi * distance) * jnp.sqrt(jnp.maximum(radial - limit, 0.0))
        )
        turns = distance * (jnp.sqrt(jnp.maximum(limit - radial, 0.0)) - wave_number)
        sine, cosine = sine_cosine(turns)
        k_real[here, :] = amplitude * cosine
        k_imag[here, :] = amplitude * sine
        return carry

    lax.fori_loop(0, RADIX, tile, 0)


def matmul(matrix, data):
    return jnp.dot(matrix[...], data, preferred_element_type=F32)


def column_pass(me, tables, wide, middle, other, k_real, k_imag, cosines, sines):
    open_ahead, ahead, back = tables
    lane = lax.broadcasted_iota(jnp.int32, (RADIX, 128), 1)
    low = lane < RADIX
    alone = (me == 0) & (lax.rem(lane, RADIX) == 0)

    def first(b, carry):
        made = matmul(open_ahead, wide[pl.ds(b, RADIX, stride=RADIX), :].astype(BF16))
        real, imag = made[:RADIX], made[RADIX:]
        cosine, sine = cosines[b], sines[b]
        middle[pl.ds(b, RADIX, stride=128), :] = real * cosine + imag * sine
        middle[pl.ds(RADIX + b, RADIX, stride=128), :] = imag * cosine - real * sine
        return carry

    lax.fori_loop(0, RADIX, first, 0, unroll=8)

    def second(k, carry):
        made = matmul(ahead, middle[pl.ds(k * 128, 128), :].astype(BF16))
        real, imag = made[:RADIX], made[RADIX:]
        real_turn, imag_turn = pltpu.roll(real, RADIX, 1), pltpu.roll(imag, RADIX, 1)
        spectrum_real = jnp.where(low, real - imag_turn, real_turn + imag)
        spectrum_imag = jnp.where(low, imag + real_turn, imag_turn - real)
        spectrum_real = jnp.where(alone, real, spectrum_real).astype(BF16).astype(F32)
        spectrum_imag = jnp.where(alone, imag, spectrum_imag).astype(BF16).astype(F32)
        here = pl.ds(k * RADIX, RADIX)
        kernel_real, kernel_imag = k_real[here, :], k_imag[here, :]
        propagated = jnp.concatenate(
            [
                spectrum_real * kernel_real - spectrum_imag * kernel_imag,
                spectrum_real * kernel_imag + spectrum_imag * kernel_real,
            ]
        )
        made = matmul(back, propagated.astype(BF16))
        real, imag = made[:RADIX], made[RADIX:]
        cosine, sine = cosines[k], sines[k]
        other[pl.ds(k, RADIX, stride=128), :] = real * cosine - imag * sine
        other[pl.ds(RADIX + k, RADIX, stride=128), :] = real * sine + imag * cosine
        return carry

    lax.fori_loop(0, RADIX, second, 0, unroll=8)

    def third(b, carry):
        made = matmul(back, other[pl.ds(b * 128, 128), :].astype(BF16))
        middle[pl.ds(b, RADIX, stride=RADIX), :] = made[:RADIX]
        middle[pl.ds(N + b, RADIX, stride=RADIX), :] = made[RADIX:]
        return carry

    lax.fori_loop(0, RADIX, third, 0, unroll=8)


def pack_blocks(middle, blocks):
    def one(yc, carry):
        for part in range(2):
            for slab in range(4):
                start = part * N + slab * 1024 + yc * 128
                for x in range(4):
                    rows = [
                        middle[pl.ds(start + zh * 32 + (x - slab) % 4 * 8, 8), :]
                        for zh in range(4)
                    ]
                    blocks[x * 8 + yc, part, slab] = jnp.concatenate(rows).astype(BF16)
        return carry

    lax.fori_loop(0, 8, one, 0)


def open_rows(s, both, gathered, middle, cosines, sines):
    real, imag = (gathered[s, part].reshape(128, 128) for part in range(2))
    which = jnp.minimum(s, 1)
    data = jnp.concatenate([real, imag], axis=1)
    made = lax.dot_general(both[which], data, NT, preferred_element_type=F32)
    for half in range(2):
        k = jnp.where(s == 0, 32, RADIX - s) if half else s
        real = made[half * RADIX : (half + 1) * RADIX]
        imag = made[128 + half * RADIX : 128 + (half + 1) * RADIX]
        cosine, sine = cosines[k], sines[k]
        middle[pl.ds(k, RADIX, stride=128), :] = real * cosine - imag * sine
        middle[pl.ds(RADIX + k, RADIX, stride=128), :] = real * sine + imag * cosine


def close_rows(back, eye, middle, wide, planes):
    def closing(b, carry):
        made = matmul(back, middle[pl.ds(b * 128, 128), :].astype(BF16))
        real, imag = made[:RADIX], made[RADIX:]
        wide[pl.ds(b, RADIX, stride=RADIX), :] = real * real + imag * imag
        return carry

    lax.fori_loop(0, RADIX, closing, 0, unroll=8)
    for t in range(32):
        block = wide[t * 128 : (t + 1) * 128, :].astype(BF16)
        made = lax.dot_general(eye[...], block, NT, preferred_element_type=F32)
        planes[:, :, t * 128 : (t + 1) * 128] = made.reshape(16, 8, 128).astype(BF16)


def edge_rows(stack, low, high):
    rows = lax.broadcasted_iota(jnp.int32, (PLANES, N), 0)
    bottom, top = jnp.zeros((PLANES, N), F32), jnp.zeros((PLANES, N), F32)
    for g in range(PLANES):
        plane = stack[g].astype(F32)
        bottom = jnp.where(rows == g, plane[0:1], bottom)
        top = jnp.where(rows == g, plane[7:8], top)
    low[...] = bottom.astype(BF16)
    high[...] = top.astype(BF16)


def inner_scores(stack, scores):
    lane = lax.broadcasted_iota(jnp.int32, (8, N), 1)

    def one(g, carry):
        centre = stack[g].astype(F32)
        lower = stack[jnp.maximum(g - 1, 0)].astype(F32)
        upper = stack[jnp.minimum(g + 1, PLANES - 1)].astype(F32)
        east = jnp.where(lane == N - 1, centre, pltpu.roll(centre, N - 1, 1))
        west = jnp.where(lane == 0, centre, pltpu.roll(centre, 1, 1))
        scores[g] = (upper - lower) * (upper - lower) + (east - west) * (east - west)
        return carry

    lax.fori_loop(0, PLANES, one, 0)


def full_scores(stack, scores, north, south, first, last, piece):
    row = lax.broadcasted_iota(jnp.int32, (8, N), 0)
    best = jnp.zeros((8, N), F32)
    norths, souths = north[...].astype(F32), south[...].astype(F32)
    for g in range(PLANES):
        centre = stack[g].astype(F32)
        before = jnp.where(first, centre[0:1], norths[g : g + 1])
        after = jnp.where(last, centre[7:8], souths[g : g + 1])
        above = jnp.where(row == 0, before, pltpu.roll(centre, 1, 0))
        below = jnp.where(row == 7, after, pltpu.roll(centre, 7, 0))
        best = jnp.maximum(best, (scores[g] + (below - above) * (below - above)) / 8.0)
    piece[...] = best.astype(BF16)


def whole_kernel(
    sections, open_ahead, ahead, back, both, eye, out,
    columns, wide, middle, other, cosines, sines, k_real, k_imag,
    blocks, staged, gathered, planes, stack, scores, low, high, north, south, piece,
    send1, recv1, send2, recv2, relay_send, relay_recv, send3, recv3, send4, recv4,
    send5, recv5, own_sem,
):
    at = {name: lax.axis_index(name) for name in AXES}
    x, y, c, zh, zl = at["x"], at["y"], at["c"], at["zh"], at["zl"]
    yc, z = y * 2 + c, zh * 4 + zl
    me, slab = x * 8 + yc, zl * 8 + yc
    xs = lax.rem(x - zl + 4, 4)
    q = (slab * 4 + zh) * 4 + xs

    def near(step, turn):
        to, layer = lax.rem(yc + step + 8, 8), lax.rem(z + turn + 16, 16)
        return {
            "zh": layer // 4,
            "x": x,
            "zl": lax.rem(layer, 4),
            "y": to // 2,
            "c": lax.rem(to, 2),
        }

    def level(dx, dy, dc):
        return {
            "zh": zh,
            "x": lax.rem(x + dx + 4, 4),
            "zl": zl,
            "y": lax.rem(y + dy + 4, 4),
            "c": lax.rem(c + dc, 2),
        }

    def number(device):
        return device["x"] * 8 + device["y"] * 2 + device["c"]

    def above(layer):
        return {**at, "zh": layer // 4, "zl": lax.rem(layer, 4)}

    def block_owner(index):
        owner = index // 16
        low_z = owner // 8
        return {
            "zh": lax.rem(index // 4, 4),
            "x": lax.rem(lax.rem(index, 4) + low_z, 4),
            "zl": low_z,
            "y": lax.rem(owner // 2, 4),
            "c": lax.rem(owner, 2),
        }

    moves = []
    for turn in (2, 1, -1, 0):
        for step in range(8):
            if (step, turn) != (0, 0):
                moves.append((step, -2 if turn == 2 and step >= 4 else turn))
    relayed, direct = [], []
    for dx in (2, 1, 3, 0):
        for dy in (2, 1, 3, 0):
            for dc in (1, 0):
                if 2 in (dx, dy):
                    side = -1 if dc else 1
                    hop = [side if d == 2 else (-1 if d == 3 else d) for d in (dx, dy)]
                    rest = [side if d == 2 else 0 for d in (dx, dy)]
                    relayed.append((hop[0], hop[1], dc, rest[0], rest[1]))
                elif (dx, dy, dc) != (0, 0, 0):
                    direct.append((-1 if dx == 3 else dx, -1 if dy == 3 else dy, dc))
    turns = (8, 7, 9, 6, 10, 5, 11, 4, 12, 3, 13, 2, 14, 1, 15)
    layers = [lax.rem(z + turn, 16) for turn in turns]
    ahead_q, behind_q = block_owner(lax.rem(q + 1, 512)), block_owner(lax.rem(q + 511, 512))

    barrier = pltpu.get_barrier_semaphore()
    everyone = [near(-step, -turn) for step, turn in moves]
    everyone += [level(dx, dy, dc) for dx in range(4) for dy in range(4) for dc in range(2)][1:]
    everyone += [above(layer) for layer in layers]
    everyone += [ahead_q, behind_q]
    for device in everyone:
        pl.semaphore_signal(barrier, inc=1, device_id=device, device_id_type=MESH)
    pl.semaphore_wait(barrier, len(everyone))

    sent = []
    for index, (step, turn) in enumerate(moves):
        sent.append(
            remote(
                sections.at[lax.rem(yc + step, 8)],
                columns.at[slab],
                send1.at[index],
                recv1.at[slab],
                near(step, turn),
            )
        )
        sent[-1].start()
    own = pltpu.make_async_copy(sections.at[yc], columns.at[slab], own_sem)
    own.start()
    make_tables(me, z, cosines, sines, k_real, k_imag)
    own.wait()
    wide[pl.ds(slab * 128, 128), :] = columns[slab].astype(F32)
    for copy in sent:
        copy.wait_send()
    for step, turn in reversed(moves):
        origin = lax.rem(lax.rem(z - turn + 16, 16), 4) * 8 + lax.rem(yc - step + 8, 8)
        slot = columns.at[origin]
        remote(slot, slot, own_sem, recv1.at[origin], near(-step, -turn)).wait_recv()
        wide[pl.ds(origin * 128, 128), :] = columns[origin].astype(F32)

    tables = (open_ahead, ahead, back)
    column_pass(me, tables, wide, middle, other, k_real, k_imag, cosines, sines)
    pack_blocks(middle, blocks)

    sent = []
    for index, (hx, hy, dc, rx, ry) in enumerate(relayed):
        target = number(level(hx + rx, hy + ry, dc))
        sent.append(
            remote(
                blocks.at[target],
                staged.at[index],
                relay_send.at[index],
                relay_recv.at[index],
                level(hx, hy, dc),
            )
        )
        sent[-1].start()
    for index, (dx, dy, dc) in enumerate(direct):
        device = level(dx, dy, dc)
        sent.append(
            remote(
                blocks.at[number(device)],
                gathered.at[me],
                send2.at[index],
                recv2.at[me],
                device,
            )
        )
        sent[-1].start()
    own = pltpu.make_async_copy(blocks.at[me], gathered.at[me], own_sem)
    own.start()
    own.wait()
    open_rows(me, both, gathered, middle, cosines, sines)
    for index, (hx, hy, dc, rx, ry) in enumerate(relayed):
        source = level(-hx, -hy, dc)
        slot = staged.at[index]
        remote(slot, slot, own_sem, relay_recv.at[index], source).wait_recv()
        sent.append(
            remote(
                slot,
                gathered.at[number(source)],
                send2.at[len(direct) + index],
                recv2.at[number(source)],
                level(rx, ry, 0),
            )
        )
        sent[-1].start()

    arrivals = [(-dx, -dy, dc) for dx, dy, dc in direct]
    arrivals += [(-hx - rx, -hy - ry, dc) for hx, hy, dc, rx, ry in relayed]
    for dx, dy, dc in arrivals:
        device = level(dx, dy, dc)
        source = number(device)
        slot = gathered.at[source]
        remote(slot, slot, own_sem, recv2.at[source], device).wait_recv()
        open_rows(source, both, gathered, middle, cosines, sines)
    for copy in sent:
        copy.wait_send()
    close_rows(back, eye, middle, wide, planes)

    def part(layer):
        return planes.at[lax.rem(layer, 4) * 4 + layer // 4]

    sent = []
    for index, layer in enumerate(layers):
        sent.append(
            remote(part(layer), stack.at[z], send3.at[index], recv3.at[z], above(layer))
        )
        sent[-1].start()
    own = pltpu.make_async_copy(part(z), stack.at[z], own_sem)
    own.start()
    own.wait()
    for copy in sent:
        copy.wait_send()
    for layer in layers:
        slot = stack.at[layer]
        remote(slot, slot, own_sem, recv3.at[layer], above(layer)).wait_recv()

    edge_rows(stack, low, high)
    sent = [
        remote(high, north, send4.at[0], recv4.at[0], ahead_q),
        remote(low, south, send4.at[1], recv4.at[1], behind_q),
    ]
    for copy in sent:
        copy.start()
    inner_scores(stack, scores)
    for copy in sent:
        copy.wait()
    full_scores(stack, scores, north, south, q == 0, q == 511, piece)

    left, right = pl.ds(0, N // 2), pl.ds(N // 2, N // 2)
    halves = (left, right)
    sent = []

    def across(step):
        return {**at, "x": lax.rem(x + step + 4, 4)}

    def along(step):
        return {**at, "zh": lax.rem(zh + step + 4, 4)}

    def row_of(place):
        return lax.rem(place - zl + 4, 4)

    def send(source, target, sem, device):
        sent.append(remote(source, target, send5.at[len(sent)], sem, device))
        sent[-1].start()

    def arrive(place, high_z, half, device):
        slot = out.at[high_z, row_of(place)]
        slot = slot if half is None else slot.at[:, halves[half]]
        sem = recv5.at[place, high_z, half or 0]
        remote(slot, slot, own_sem, sem, device).wait_recv()

    for step in (1, -1):
        send(piece, out.at[zh, xs], recv5.at[x, zh, 0], along(step))
    for step in (1, -1):
        send(piece, out.at[zh, xs], recv5.at[x, zh, 0], across(step))
    own = pltpu.make_async_copy(piece, out.at[zh, xs], own_sem)
    own.start()
    for half, step in enumerate((1, -1)):
        from_z = lax.rem(zh - step + 4, 4)
        arrive(x, from_z, None, along(-step))
        slot = out.at[from_z, xs, :, halves[half]]
        send(slot, slot, recv5.at[x, from_z, half], along(step))
        for turn in (1, -1):
            slot = out.at[from_z, xs]
            send(slot, slot, recv5.at[x, from_z, 0], across(turn))
    far_z = lax.rem(zh + 2, 4)
    for high_z in (zh, lax.rem(zh + 3, 4), lax.rem(zh + 1, 4), far_z):
        if high_z is far_z:
            for half, step in enumerate((1, -1)):
                arrive(x, far_z, half, along(-step))
            for turn in (1, -1):
                slot = out.at[far_z, xs]
                send(slot, slot, recv5.at[x, far_z, 0], across(turn))
        for half, step in enumerate((1, -1)):
            place = lax.rem(x - step + 4, 4)
            arrive(place, high_z, None, across(-step))
            slot = out.at[high_z, row_of(place), :, halves[half]]
            send(slot, slot, recv5.at[place, high_z, half], across(step))
    for high_z in (zh, lax.rem(zh + 3, 4), lax.rem(zh + 1, 4), far_z):
        for half, step in enumerate((1, -1)):
            arrive(lax.rem(x + 2, 4), high_z, half, across(-step))
    own.wait()
    for copy in sent:
        copy.wait_send()


def shards(hologram, background):
    contrast = (hologram.astype(F32) / background.astype(F32) - 1.0).astype(BF16)
    sections = row_sections(contrast, lax.axis_index("x"))
    vmem, dma = pltpu.VMEM, pltpu.SemaphoreType.DMA
    table = vmem((RADIX, RADIX, 128), F32)
    merged = pl.pallas_call(
        whole_kernel,
        name="whole",
        out_shape=jax.ShapeDtypeStruct((4, 4, 8, N), BF16),
        in_specs=[pl.BlockSpec(memory_space=vmem)] * 6,
        out_specs=pl.BlockSpec(memory_space=vmem),
        scratch_shapes=[
            vmem((32, 128, 128), BF16),
            vmem((N, 128), F32),
            vmem((2 * N, 128), F32),
            vmem((2 * N, 128), F32),
            table,
            table,
            vmem((N, 128), F32),
            vmem((N, 128), F32),
            vmem((32, 2, 4, 32, 128), BF16),
            vmem((14, 2, 4, 32, 128), BF16),
            vmem((32, 2, 4, 32, 128), BF16),
            vmem((16, 8, N), BF16),
            vmem((PLANES, 8, N), BF16),
            vmem((PLANES, 8, N), F32),
            *[vmem((PLANES, N), BF16)] * 4,
            vmem((8, N), BF16),
            dma((31,)),
            dma((32,)),
            dma((31,)),
            dma((32,)),
            dma((14,)),
            dma((14,)),
            dma((15,)),
            dma((16,)),
            dma((2,)),
            dma((2,)),
            dma((20,)),
            dma((4, 4, 2)),
            dma,
        ],
        compiler_params=pltpu.CompilerParams(
            collective_id=0, has_side_effects=True, vmem_limit_bytes=56 << 20
        ),
    )(sections, *pass_tables())
    return merged.reshape(128, N).astype(F32)


def solution(mesh):
    fine = Mesh(mesh.devices.reshape(SIZES), AXES)
    spec = P(("zl", "y", "c"), None)
    return jax.shard_map(
        shards, mesh=fine, in_specs=(spec, spec), out_specs=spec, check_vma=False
    )
```

time: 718 us -> 175 us (0.24)
  the two profiles are of different devices: /device:TPU:8 before, /device:TPU:2 now
where the time goes in v2:
time: 175 us
  Pallas kernels  164 us (94%)
  other arithmetic  5.7 us (3%)
  local copies, waits for them, and re-layouts  4.53 us (3%)
    pallas_call x1, Pallas kernels, shards(): pl.pallas_call(whole_kernel, name='whole', out_shape=jax.ShapeDtypeStruct...  164 us

profile of v2, /device:TPU:2, one launch (start us, length us, event | category | flops | bytes accessed | tf_op | source)
XLA Modules:
  0.0 175.2 jit_solution(8295367158404073324)
XLA Ops:
  0.0 0.0 copy-start
  0.0 0.8 dynamic-slice_bitcast_fusion
  0.8 0.7 constant_dynamic-slice_fusion
  1.5 0.7 pad_maximum_fusion.2
  2.1 0.7 pad_maximum_fusion.1
  2.8 0.1 copy.26
  2.9 0.1 copy.27
  3.0 1.6 copy.23
  4.6 0.0 copy-done
  4.6 0.7 copy.24
  5.3 0.0 copy-start.2
  5.3 0.4 add_convert_fusion
  5.7 0.2 copy-done.2
  6.0 0.0 copy-start.1
  6.0 0.8 fusion.1
  6.8 0.3 subtract_convert_fusion
  7.1 0.1 maximum_bitcast_fusion
  7.2 0.0 copy-done.1
  7.2 0.3 fusion
  7.7 0.2 copy.31
  7.8 0.1 copy.30
  8.0 0.7 pad_maximum_fusion.sections
  8.7 163.7 %whole.1 = bf16[4,4,8,4096]{3,2,1,0:T(8,128)(2,1)} custom-call(bf16[8,128,128]{2,1,0:T(8,128)(2,1)} %pad_maximum_fusion.sections, bf16[128,64]{1,0:T(8,128)(2,1)} %constant.35.clone.open_ahead, bf16[128,128]{1,0:T(8,128)(2,1)} %constant.36.clone.ahead, bf16[128,128]{1,0:T(8,128)(2,1)} %constant.37.clone.back, bf16[2,256,256]{2,1,0:T(8,128)(2,1)} %constant.38.clone.both, ...), custom_call_target="tpu_custom_call" | custom-call | tf_op jit(solution)/shard_map/whole/pallas_call | solution.py:547
  172.4 2.8 %bitcast_convert_fusion = f32[128,4096]{1,0:T(8,128)} fusion(bf16[4,4,8,4096]{3,2,1,0:T(8,128)(2,1)} %whole.1), kind=kLoop, calls=%fused_computation.3 | loop fusion | flops 524288 | bytes 3145728 | tf_op jit(solution)/shard_map/convert_element_type | solution.py:588
  (7 shorter events, 0.1 us)
Async XLA Ops:
  0.0 4.6 %copy-start = (bf16[128,4096]{1,0:T(8,128)(2,1)S(1)}, bf16[128,4096]{1,0:T(8,128)(2,1)}, u32[]{:S(2)}) copy-start(bf16[128,4096]{1,0:T(8,128)(2,1)} %param.11) | copy-start | bytes 3145732
  5.3 0.7 copy-start.2
  6.0 1.3 copy-start.1

commit v3 on v2

v3 whole, which is shorter than its diff:
```python
import math

import jax
import jax.numpy as jnp
import numpy as np
from jax import lax
from jax.experimental import pallas as pl
from jax.experimental.pallas import tpu as pltpu
from jax.sharding import Mesh
from jax.sharding import PartitionSpec as P

N = 4096
RADIX = 64
PLANES = 16
WIDE = 72
DEEP = 136
HALF = N // 2
AXES = ("zh", "x", "zl", "y", "c")
SIZES = (4, 4, 4, 4, 2)
MESH = pl.DeviceIdType.MESH
NT = (((1,), (1,)), ((), ()))
F32 = jnp.float32
BF16 = jnp.bfloat16

wave_number = 0.6
depth_start = 8.0
depth_step = 2.0


def fourier_tables(sign_value):
    indices = np.arange(RADIX)
    angles = (indices[:, None] * indices[None, :] % RADIX) * (sign_value * 2.0 * math.pi / RADIX)
    real, imag = np.cos(angles) / math.sqrt(RADIX), np.sin(angles) / math.sqrt(RADIX)
    matrix = np.stack([np.stack([real, -imag]), np.stack([imag, real])])
    return matrix.astype(np.float32)


def twiddle_table(sign_value):
    indices = np.arange(RADIX)
    angles = (indices[:, None] * indices[None, :]) * (sign_value * 2.0 * math.pi / N)
    return np.cos(angles).astype(np.float32), np.sin(angles).astype(np.float32)


def pass_tables():
    ahead, back = fourier_tables(-1.0), fourier_tables(1.0)
    flat = lambda table: table.transpose(0, 2, 1, 3).reshape(128, 128)
    natural = np.eye(128, dtype=np.float32).reshape(2, 2, 32, 128).swapaxes(0, 1).reshape(128, 128)
    both = np.zeros((2, 2, 2, RADIX, 2, 128), np.float32)
    for lane in range(128):
        far, j = divmod(lane, RADIX)
        both[1, :, far, :, :, lane] = back[:, :, :, RADIX - 1 - j if far else j].transpose(0, 2, 1)
        if j >= RADIX // 2:
            half, j = 1, (95 - j if far else j - 32)
        else:
            half, j = 0, ((RADIX - j if j else 32) if far else j)
        both[0, :, half, :, :, lane] = back[:, :, :, j].transpose(0, 2, 1)
    tables = (
        flat(ahead),
        flat(back),
        both.reshape(2, 256, 256),
        np.eye(128, dtype=np.float32),
        natural,
    )
    return [jnp.asarray(ahead[:, 0].reshape(128, RADIX), F32)] + [
        jnp.asarray(table, BF16) for table in tables
    ]


def row_pass(x, hologram, background, open_exact, ahead, eye, wide, middle, sections):
    for t in range(32):
        here = slice(t * 128, (t + 1) * 128)
        ratio = hologram[:, here].astype(F32) / background[:, here].astype(F32)
        contrast = (ratio - 1.0).astype(BF16)
        made = lax.dot_general(eye[...], contrast, NT, preferred_element_type=F32)
        wide[2 * t * WIDE : 2 * t * WIDE + RADIX, :] = made[:RADIX]
        wide[(2 * t + 1) * WIDE : (2 * t + 1) * WIDE + RADIX, :] = made[RADIX:]
    own = pl.multiple_of(x * 8, 8)
    chosen = [open_exact[pl.ds(own, 8), :], open_exact[32:40, :]]
    chosen += [open_exact[pl.ds(RADIX + own, 8), :], open_exact[RADIX + 32 : RADIX + 40, :]]
    matrix = jnp.concatenate(chosen).astype(BF16)
    row = lax.broadcasted_iota(jnp.int32, (16, 128), 0)
    k = jnp.where(row < 8, x * 8 + row, row + 24).astype(F32)

    def opening(b, carry):
        data = wide[pl.ds(b, RADIX, stride=WIDE), :].astype(BF16)
        made = jnp.dot(matrix, data, preferred_element_type=F32)
        real, imag = made[:16], made[16:]
        sine, cosine = sine_cosine(k * (b.astype(F32) / N))
        middle[pl.ds(b, 16, stride=DEEP), :] = real * cosine + imag * sine
        middle[pl.ds(RADIX + b, 16, stride=DEEP), :] = imag * cosine - real * sine
        return carry

    lax.fori_loop(0, RADIX, opening, 0, unroll=8)

    def section(index):
        made = matmul(ahead, middle[index * DEEP : index * DEEP + 128, :].astype(BF16))
        return lax.dot_general(eye[...], made.astype(BF16), NT, preferred_element_type=F32)

    lane = lax.broadcasted_iota(jnp.int32, (128, 128), 1)
    zero, half = section(0), section(8)
    turned = pltpu.roll(zero, 32, 1)
    packed = jnp.where(lax.rem(lane, RADIX) >= 32, pltpu.roll(half, 32, 1), zero)
    packed = jnp.where(lane == RADIX, turned, packed)
    sections[0] = jnp.where(x == 0, packed, zero).astype(BF16)
    for index in range(1, 8):
        sections[index] = section(index).astype(BF16)


def remote(source, target, send_sem, recv_sem, device):
    return pltpu.make_async_remote_copy(
        src_ref=source,
        dst_ref=target,
        send_sem=send_sem,
        recv_sem=recv_sem,
        device_id=device,
        device_id_type=MESH,
    )


def sine_cosine(turns):
    half = (turns - jnp.floor(turns + 0.5)) * math.pi
    square = half * half
    sine, cosine = jnp.zeros_like(half), jnp.zeros_like(half)
    for power in range(6, -1, -1):
        cosine = cosine * square + (-1) ** power / math.factorial(2 * power)
        if power < 6:
            sine = sine * square + (-1) ** power / math.factorial(2 * power + 1)
    sine = sine * half
    return 2.0 * sine * cosine, 1.0 - 2.0 * sine * sine


def make_tables(me, z, cosines, sines, k_real, k_imag):
    distance = depth_start + depth_step * z.astype(F32)
    lane = lax.broadcasted_iota(jnp.int32, (RADIX, 128), 1)
    row = lax.broadcasted_iota(jnp.int32, (RADIX, 128), 0)
    j = lax.rem(lane, RADIX)
    general = me + RADIX * j
    lone = jnp.where(j == 0, jnp.where(lane >= RADIX, N // 2, 0), RADIX * j)
    lone = jnp.where(j >= RADIX // 2, 32 + RADIX * (j - RADIX // 2), lone)
    natural = jnp.where(me == 0, lone, general)
    freq = jnp.where(natural >= N // 2, natural - N, natural).astype(F32) / N
    column_part = freq * freq
    base = jnp.where(row >= RADIX // 2, RADIX * row - N, RADIX * row)
    limit = wave_number * wave_number

    def tile(k, carry):
        here = pl.ds(k * RADIX, RADIX)
        sine, cosine = sine_cosine((row * k).astype(F32) / N)
        cosines[k], sines[k] = cosine, sine
        freq = (base + k).astype(F32) / N
        radial = freq * freq + column_part
        amplitude = jnp.exp(
            (-2.0 * math.pi * distance) * jnp.sqrt(jnp.maximum(radial - limit, 0.0))
        )
        turns = distance * (jnp.sqrt(jnp.maximum(limit - radial, 0.0)) - wave_number)
        sine, cosine = sine_cosine(turns)
        k_real[here, :] = amplitude * cosine
        k_imag[here, :] = amplitude * sine
        return carry

    lax.fori_loop(0, RADIX, tile, 0)


def widen(slab, columns, wide):
    for half in range(2):
        rows = columns[slab, pl.ds(half * RADIX, RADIX), :]
        wide[pl.ds((2 * slab + half) * WIDE, RADIX), :] = rows.astype(F32)


def matmul(matrix, data):
    return jnp.dot(matrix[...], data, preferred_element_type=F32)


def matmul_right(data, matrix):
    return jnp.dot(data, matrix[...], preferred_element_type=F32)


def column_pass(me, tables, wide, middle, other, k_real, k_imag, cosines, sines):
    open_exact, ahead, back = tables
    lane = lax.broadcasted_iota(jnp.int32, (RADIX, 128), 1)
    low = lane < RADIX
    alone = (me == 0) & (lax.rem(lane, RADIX) == 0)

    open_ahead = open_exact[...].astype(BF16)

    def first(b, carry):
        made = matmul(open_ahead, wide[pl.ds(b, RADIX, stride=WIDE), :].astype(BF16))
        real, imag = made[:RADIX], made[RADIX:]
        cosine, sine = cosines[b], sines[b]
        middle[pl.ds(b, RADIX, stride=DEEP), :] = real * cosine + imag * sine
        middle[pl.ds(RADIX + b, RADIX, stride=DEEP), :] = imag * cosine - real * sine
        return carry

    lax.fori_loop(0, RADIX, first, 0, unroll=8)

    def second(k, carry):
        made = matmul(ahead, middle[pl.ds(k * DEEP, 128), :].astype(BF16))
        real, imag = made[:RADIX], made[RADIX:]
        real_turn, imag_turn = pltpu.roll(real, RADIX, 1), pltpu.roll(imag, RADIX, 1)
        spectrum_real = jnp.where(low, real - imag_turn, real_turn + imag)
        spectrum_imag = jnp.where(low, imag + real_turn, imag_turn - real)
        spectrum_real = jnp.where(alone, real, spectrum_real).astype(BF16).astype(F32)
        spectrum_imag = jnp.where(alone, imag, spectrum_imag).astype(BF16).astype(F32)
        here = pl.ds(k * RADIX, RADIX)
        kernel_real, kernel_imag = k_real[here, :], k_imag[here, :]
        propagated = jnp.concatenate(
            [
                spectrum_real * kernel_real - spectrum_imag * kernel_imag,
                spectrum_real * kernel_imag + spectrum_imag * kernel_real,
            ]
        )
        made = matmul(back, propagated.astype(BF16))
        real, imag = made[:RADIX], made[RADIX:]
        cosine, sine = cosines[k], sines[k]
        other[pl.ds(k, RADIX, stride=DEEP), :] = real * cosine - imag * sine
        other[pl.ds(RADIX + k, RADIX, stride=DEEP), :] = real * sine + imag * cosine
        return carry

    lax.fori_loop(0, RADIX, second, 0, unroll=8)

    def third(b, carry):
        made = matmul(back, other[pl.ds(b * DEEP, 128), :].astype(BF16))
        middle[pl.ds(b, RADIX, stride=WIDE), :] = made[:RADIX]
        middle[pl.ds(RADIX * WIDE + b, RADIX, stride=WIDE), :] = made[RADIX:]
        return carry

    lax.fori_loop(0, RADIX, third, 0, unroll=8)


def block_rows(middle, part, x, yc):
    rows = []
    for low_z in range(4):
        start = (part * RADIX + low_z * 16 + yc * 2) * WIDE + lax.rem(x - low_z + 4, 4) * 8
        for zh in range(4):
            offset = pl.multiple_of(start + zh // 2 * WIDE + zh % 2 * 32, 8)
            rows.append(middle[pl.ds(offset, 8), :])
    return jnp.concatenate(rows).astype(BF16)


def partner(k):
    return jnp.where(k == 0, 32, RADIX - k)


def make_block(me, target, both, middle, cosines, sines, blocks):
    x, yc = target // 8, lax.rem(target, 8)
    data = jnp.concatenate([block_rows(middle, part, x, yc) for part in range(2)], axis=1)
    made = lax.dot_general(both[jnp.minimum(me, 1)], data, NT, preferred_element_type=F32)
    for half in range(2):
        k = partner(me) if half else me
        real = made[half * RADIX : (half + 1) * RADIX]
        imag = made[128 + half * RADIX : 128 + (half + 1) * RADIX]
        cosine, sine = cosines[k], sines[k]
        turned = (real * cosine - imag * sine, real * sine + imag * cosine)
        for part in range(2):
            for chunk in range(2):
                rows = turned[part][chunk * 32 : (chunk + 1) * 32]
                blocks[target, chunk, part * 2 + half] = rows.astype(BF16)


def place_block(source, chunk, gathered, other):
    for part in range(2):
        for half in range(2):
            k = partner(source) if half else source
            rows = gathered[source, chunk, part * 2 + half].astype(F32)
            start = chunk * 32 * DEEP + part * RADIX + k
            other[pl.ds(start, 32, stride=DEEP), :] = rows


def close_rows(chunk, back, eye, other, wide, planes):
    def closing(index, carry):
        b = chunk * 32 + index
        made = matmul(back, other[pl.ds(b * DEEP, 128), :].astype(BF16))
        real, imag = made[:RADIX], made[RADIX:]
        wide[pl.ds(b, RADIX, stride=WIDE), :] = real * real + imag * imag
        return carry

    lax.fori_loop(0, 32, closing, 0, unroll=8)
    for t in range(16):
        rows = [
            wide[a * WIDE + chunk * 32 : a * WIDE + chunk * 32 + 32, :]
            for a in range(4 * t, 4 * t + 4)
        ]
        block = jnp.concatenate(rows).astype(BF16)
        made = lax.dot_general(eye[...], block, NT, preferred_element_type=F32)
        here = slice(t * 128, (t + 1) * 128)
        planes[chunk, :, :, here] = made.reshape(16, 8, 128).astype(BF16)


def edge_rows(chunk, stack, low, high):
    rows = lax.broadcasted_iota(jnp.int32, (PLANES, HALF), 0)
    bottom, top = jnp.zeros((PLANES, HALF), F32), jnp.zeros((PLANES, HALF), F32)
    for g in range(PLANES):
        plane = stack[chunk, g].astype(F32)
        bottom = jnp.where(rows == g, plane[0:1], bottom)
        top = jnp.where(rows == g, plane[7:8], top)
    low[chunk] = bottom.astype(BF16)
    high[chunk] = top.astype(BF16)


def depth_scores(chunk, stack, scores):
    def one(g, carry):
        lower = stack[chunk, jnp.maximum(g - 1, 0)].astype(F32)
        upper = stack[chunk, jnp.minimum(g + 1, PLANES - 1)].astype(F32)
        scores[chunk, g] = (upper - lower) * (upper - lower)
        return carry

    lax.fori_loop(0, PLANES, one, 0, unroll=2)


def row_scores(chunk, stack, scores, north, south, first, last):
    row = lax.broadcasted_iota(jnp.int32, (8, HALF), 0)
    norths, souths = north[chunk].astype(F32), south[chunk].astype(F32)
    for g in range(PLANES):
        centre = stack[chunk, g].astype(F32)
        before = jnp.where(first, centre[0:1], norths[g : g + 1])
        after = jnp.where(last, centre[7:8], souths[g : g + 1])
        above = jnp.where(row == 0, before, pltpu.roll(centre, 1, 0))
        below = jnp.where(row == 7, after, pltpu.roll(centre, 7, 0))
        scores[chunk, g] = scores[chunk, g] + (below - above) * (below - above)


def side_scores(stack, scores):
    lane = lax.broadcasted_iota(jnp.int32, (8, HALF), 1)
    start, end = lax.rem(lane, 32) == 0, lax.rem(lane, 32) == 31

    def one(g, carry):
        left, right = stack[0, g].astype(F32), stack[1, g].astype(F32)
        left_before, left_after = pltpu.roll(left, 1, 1), pltpu.roll(left, HALF - 1, 1)
        right_before, right_after = pltpu.roll(right, 1, 1), pltpu.roll(right, HALF - 1, 1)
        west = jnp.where(start, jnp.where(lane == 0, left, right_before), left_before)
        east = jnp.where(end, pltpu.roll(right, 31, 1), left_after)
        scores[0, g] = scores[0, g] + (east - west) * (east - west)
        west = jnp.where(start, pltpu.roll(left, HALF - 31, 1), right_before)
        east = jnp.where(end, jnp.where(lane == HALF - 1, right, left_after), right_after)
        scores[1, g] = scores[1, g] + (east - west) * (east - west)
        return carry

    lax.fori_loop(0, PLANES, one, 0)


def sharpest(scores, natural, piece):
    best = [jnp.max(scores[chunk], axis=0) / 8.0 for chunk in range(2)]
    lane = lax.broadcasted_iota(jnp.int32, (8, 128), 1)
    tiles = []
    for t in range(16):
        here = slice(t * 128, (t + 1) * 128)
        first, second = best[0][:, here], best[1][:, here]
        tiles.append(jnp.where(lane < RADIX, first, pltpu.roll(second, RADIX, 1)))
        tiles.append(jnp.where(lane < RADIX, pltpu.roll(first, RADIX, 1), second))
    made = matmul_right(jnp.concatenate(tiles).astype(BF16), natural)
    for t in range(32):
        piece[:, t * 128 : (t + 1) * 128] = made[t * 8 : (t + 1) * 8].astype(BF16)


def whole_kernel(
    hologram, background, open_exact, ahead, back, both, eye, natural, out,
    sections, columns, passing, wide, middle, other, cosines, sines, k_real, k_imag,
    blocks, staged, gathered, planes, opposite, stack, scores, low, high, north, south, piece,
    send1, recv1, relay1_send, relay1_recv, send2, recv2, relay_send, relay_recv,
    send3, recv3, far_send, far_recv, send4, recv4, send5, recv5, own_sem,
):
    at = {name: lax.axis_index(name) for name in AXES}
    x, y, c, zh, zl = at["x"], at["y"], at["c"], at["zh"], at["zl"]
    yc, z = y * 2 + c, zh * 4 + zl
    me, slab = x * 8 + yc, zl * 8 + yc
    xs = lax.rem(x - zl + 4, 4)
    q = (slab * 4 + zh) * 4 + xs

    def near(dy, dc, turn):
        layer = lax.rem(z + turn + 16, 16)
        return {
            "zh": layer // 4,
            "x": x,
            "zl": lax.rem(layer, 4),
            "y": lax.rem(y + dy + 4, 4),
            "c": lax.rem(c + dc, 2),
        }

    def level(dx, dy, dc):
        return {
            "zh": zh,
            "x": lax.rem(x + dx + 4, 4),
            "zl": zl,
            "y": lax.rem(y + dy + 4, 4),
            "c": lax.rem(c + dc, 2),
        }

    def number(device):
        return device["x"] * 8 + device["y"] * 2 + device["c"]

    def slab_of(device):
        return device["zl"] * 8 + device["y"] * 2 + device["c"]

    def above(layer):
        return {**at, "zh": layer // 4, "zl": lax.rem(layer, 4)}

    def up(turn):
        return lax.rem(z + turn + 16, 16)

    def block_owner(index):
        owner = index // 16
        low_z = owner // 8
        return {
            "zh": lax.rem(index // 4, 4),
            "x": lax.rem(lax.rem(index, 4) + low_z, 4),
            "zl": low_z,
            "y": lax.rem(owner // 2, 4),
            "c": lax.rem(owner, 2),
        }

    moves, hops = [], []
    for turn in (2, 1, -1, 0):
        for dc in (1, 0):
            toward = -2 if turn == 2 and dc else turn
            hops.append((-1 if dc else 1, dc, toward))
            for dy in (1, -1, 0):
                if (dy, dc, turn) != (0, 0, 0):
                    moves.append((dy, dc, toward))
    relayed, direct = [], []
    for dx in (2, 1, 3, 0):
        for dy in (2, 1, 3, 0):
            for dc in (1, 0):
                if 2 in (dx, dy):
                    side = -1 if dc else 1
                    hop = [side if d == 2 else (-1 if d == 3 else d) for d in (dx, dy)]
                    rest = [side if d == 2 else 0 for d in (dx, dy)]
                    relayed.append((hop[0], hop[1], dc, rest[0], rest[1]))
                elif (dx, dy, dc) != (0, 0, 0):
                    direct.append((-1 if dx == 3 else dx, -1 if dy == 3 else dy, dc))
    turns = (7, -7, 6, -6, 5, -5, 4, -4, 3, -3, 2, -2, 1, -1)
    ahead_q, behind_q = block_owner(lax.rem(q + 1, 512)), block_owner(lax.rem(q + 511, 512))

    barrier = pltpu.get_barrier_semaphore()
    everyone = [near(-dy, dc, -turn) for dy, dc, turn in moves + hops]
    everyone += [level(dx, dy, dc) for dx in range(4) for dy in range(4) for dc in range(2)][1:]
    everyone += [above(up(turn)) for turn in turns]
    everyone += [ahead_q, behind_q]
    for device in everyone:
        pl.semaphore_signal(barrier, inc=1, device_id=device, device_id_type=MESH)
    row_pass(x, hologram, background, open_exact, ahead, eye, wide, middle, sections)
    pl.semaphore_wait(barrier, len(everyone))

    sent = []
    for index, (side, dc, turn) in enumerate(hops):
        target = near(2, dc, turn)
        sent.append(
            remote(
                sections.at[target["y"] * 2 + target["c"]],
                passing.at[index],
                relay1_send.at[index],
                relay1_recv.at[index],
                near(side, dc, turn),
            )
        )
        sent[-1].start()
    for index, (dy, dc, turn) in enumerate(moves):
        target = near(dy, dc, turn)
        sent.append(
            remote(
                sections.at[target["y"] * 2 + target["c"]],
                columns.at[slab],
                send1.at[index],
                recv1.at[slab],
                target,
            )
        )
        sent[-1].start()
    own = pltpu.make_async_copy(sections.at[yc], columns.at[slab], own_sem)
    own.start()
    make_tables(me, z, cosines, sines, k_real, k_imag)
    own.wait()
    widen(slab, columns, wide)
    for index, (side, dc, turn) in enumerate(hops):
        source = near(-side, dc, -turn)
        slot = passing.at[index]
        remote(slot, slot, own_sem, relay1_recv.at[index], source).wait_recv()
        sent.append(
            remote(
                slot,
                columns.at[slab_of(source)],
                send1.at[len(moves) + index],
                recv1.at[slab_of(source)],
                level(0, side, 0),
            )
        )
        sent[-1].start()
    arrivals = [(-dy, dc, -turn) for dy, dc, turn in reversed(moves)]
    arrivals += [(2, dc, -turn) for side, dc, turn in hops]
    for dy, dc, turn in arrivals:
        source = near(dy, dc, turn)
        origin = slab_of(source)
        slot = columns.at[origin]
        remote(slot, slot, own_sem, recv1.at[origin], source).wait_recv()
        widen(origin, columns, wide)
    for copy in sent:
        copy.wait_send()

    tables = (open_exact, ahead, back)
    column_pass(me, tables, wide, middle, other, k_real, k_imag, cosines, sines)

    sent = []

    def send_relayed(chunk, index):
        hx, hy, dc, rx, ry = relayed[index]
        sent.append(
            remote(
                blocks.at[number(level(hx + rx, hy + ry, dc)), chunk],
                staged.at[chunk, index],
                relay_send.at[chunk, index],
                relay_recv.at[chunk, index],
                level(hx, hy, dc),
            )
        )
        sent[-1].start()

    def send_direct(chunk, index):
        device = level(*direct[index])
        sent.append(
            remote(
                blocks.at[number(device), chunk],
                gathered.at[me, chunk],
                send2.at[chunk, index],
                recv2.at[me, chunk],
                device,
            )
        )
        sent[-1].start()

    def make(device):
        make_block(me, number(device), both, middle, cosines, sines, blocks)

    for index, (hx, hy, dc, rx, ry) in enumerate(relayed):
        make(level(hx + rx, hy + ry, dc))
        if index % 2:
            send_relayed(0, index - 1)
            send_relayed(0, index)
    for index, offset in enumerate(direct):
        make(level(*offset))
        if index % 2:
            send_direct(0, index - 1)
            send_direct(0, index)
    send_direct(0, len(direct) - 1)
    for index in range(len(relayed)):
        send_relayed(1, index)
    for index in range(len(direct)):
        send_direct(1, index)
    make(level(0, 0, 0))
    own = pltpu.make_async_copy(blocks.at[me], gathered.at[me], own_sem)
    own.start()
    own.wait()

    def part(chunk, layer):
        return planes.at[chunk, lax.rem(layer, 4) * 4 + layer // 4]

    lanes = (pl.ds(0, HALF // 2), pl.ds(HALF // 2, HALF // 2))

    def forward_far(chunk):
        for side, turn in enumerate((4, -4)):
            slot = opposite.at[chunk, side]
            remote(slot, slot, own_sem, far_recv.at[chunk, side], above(up(-turn))).wait_recv()
            sent.append(
                remote(
                    slot,
                    stack.at[chunk, up(-turn), :, lanes[side]],
                    far_send.at[chunk, 2 + side],
                    recv3.at[chunk, up(-turn), side],
                    above(up(turn)),
                )
            )
            sent[-1].start()

    for chunk in range(2):
        for index, (hx, hy, dc, rx, ry) in enumerate(relayed):
            source = level(-hx, -hy, dc)
            slot = staged.at[chunk, index]
            remote(slot, slot, own_sem, relay_recv.at[chunk, index], source).wait_recv()
            sent.append(
                remote(
                    slot,
                    gathered.at[number(source), chunk],
                    send2.at[chunk, len(direct) + index],
                    recv2.at[number(source), chunk],
                    level(rx, ry, 0),
                )
            )
            sent[-1].start()
        place_block(me, chunk, gathered, other)
        arrivals = [(-dx, -dy, dc) for dx, dy, dc in direct]
        arrivals += [(-hx - rx, -hy - ry, dc) for hx, hy, dc, rx, ry in relayed]
        for dx, dy, dc in arrivals:
            device = level(dx, dy, dc)
            source = number(device)
            slot = gathered.at[source, chunk]
            remote(slot, slot, own_sem, recv2.at[source, chunk], device).wait_recv()
            place_block(source, chunk, gathered, other)
        close_rows(chunk, back, eye, other, wide, planes)
        if chunk:
            forward_far(0)
        far = up(8)
        for side, turn in enumerate((4, -4)):
            sent.append(
                remote(
                    part(chunk, far).at[:, lanes[side]],
                    opposite.at[chunk, side],
                    far_send.at[chunk, side],
                    far_recv.at[chunk, side],
                    above(up(turn)),
                )
            )
            sent[-1].start()
        for index, turn in enumerate(turns):
            layer = up(turn)
            sent.append(
                remote(
                    part(chunk, layer),
                    stack.at[chunk, z],
                    send3.at[chunk, index],
                    recv3.at[chunk, z, 0],
                    above(layer),
                )
            )
            sent[-1].start()
        own = pltpu.make_async_copy(part(chunk, z), stack.at[chunk, z], own_sem)
        own.start()
        own.wait()
    forward_far(1)

    def edges(chunk):
        edge_rows(chunk, stack, low, high)
        pair = [
            remote(
                high.at[chunk], north.at[chunk],
                send4.at[chunk, 0], recv4.at[chunk, 0], ahead_q,
            ),
            remote(
                low.at[chunk], south.at[chunk],
                send4.at[chunk, 1], recv4.at[chunk, 1], behind_q,
            ),
        ]
        for copy in pair:
            copy.start()
        return pair

    for chunk in range(2):
        for turn in reversed(turns):
            slot = stack.at[chunk, up(turn)]
            remote(slot, slot, own_sem, recv3.at[chunk, up(turn), 0], above(up(turn))).wait_recv()
        for side, turn in enumerate((-4, 4)):
            slot = stack.at[chunk, up(8), :, lanes[side]]
            remote(slot, slot, own_sem, recv3.at[chunk, up(8), side], above(up(turn))).wait_recv()
        pair = edges(chunk)
        depth_scores(chunk, stack, scores)
        if chunk:
            side_scores(stack, scores)
        for copy in pair:
            copy.wait()
        row_scores(chunk, stack, scores, north, south, q == 0, q == 511)
    for copy in sent:
        copy.wait_send()
    sharpest(scores, natural, piece)

    left, right = pl.ds(0, N // 2), pl.ds(N // 2, N // 2)
    halves = (left, right)
    sent = []

    def across(step):
        return {**at, "x": lax.rem(x + step + 4, 4)}

    def along(step):
        return {**at, "zh": lax.rem(zh + step + 4, 4)}

    def row_of(place):
        return lax.rem(place - zl + 4, 4)

    def send(source, target, sem, device):
        sent.append(remote(source, target, send5.at[len(sent)], sem, device))
        sent[-1].start()

    def arrive(place, high_z, half, device):
        slot = out.at[high_z, row_of(place)]
        slot = slot if half is None else slot.at[:, halves[half]]
        sem = recv5.at[place, high_z, half or 0]
        remote(slot, slot, own_sem, sem, device).wait_recv()

    for step in (1, -1):
        send(piece, out.at[zh, xs], recv5.at[x, zh, 0], along(step))
    for step in (1, -1):
        send(piece, out.at[zh, xs], recv5.at[x, zh, 0], across(step))
    own = pltpu.make_async_copy(piece, out.at[zh, xs], own_sem)
    own.start()
    for half, step in enumerate((1, -1)):
        from_z = lax.rem(zh - step + 4, 4)
        arrive(x, from_z, None, along(-step))
        slot = out.at[from_z, xs, :, halves[half]]
        send(slot, slot, recv5.at[x, from_z, half], along(step))
        for turn in (1, -1):
            slot = out.at[from_z, xs]
            send(slot, slot, recv5.at[x, from_z, 0], across(turn))
    far_z = lax.rem(zh + 2, 4)
    for high_z in (zh, lax.rem(zh + 3, 4), lax.rem(zh + 1, 4), far_z):
        if high_z is far_z:
            for half, step in enumerate((1, -1)):
                arrive(x, far_z, half, along(-step))
            for turn in (1, -1):
                slot = out.at[far_z, xs]
                send(slot, slot, recv5.at[x, far_z, 0], across(turn))
        for half, step in enumerate((1, -1)):
            place = lax.rem(x - step + 4, 4)
            arrive(place, high_z, None, across(-step))
            slot = out.at[high_z, row_of(place), :, halves[half]]
            send(slot, slot, recv5.at[place, high_z, half], across(step))
    for high_z in (zh, lax.rem(zh + 3, 4), lax.rem(zh + 1, 4), far_z):
        for half, step in enumerate((1, -1)):
            arrive(lax.rem(x + 2, 4), high_z, half, across(-step))
    own.wait()
    for copy in sent:
        copy.wait_send()


def shards(hologram, background):
    vmem, dma = pltpu.VMEM, pltpu.SemaphoreType.DMA
    table = vmem((RADIX, RADIX, 128), F32)
    merged = pl.pallas_call(
        whole_kernel,
        name="whole",
        out_shape=jax.ShapeDtypeStruct((4, 4, 8, N), BF16),
        in_specs=[pl.BlockSpec(memory_space=vmem)] * 8,
        out_specs=pl.BlockSpec(memory_space=vmem),
        scratch_shapes=[
            vmem((8, 128, 128), BF16),
            vmem((32, 128, 128), BF16),
            vmem((8, 128, 128), BF16),
            vmem((RADIX * WIDE, 128), F32),
            vmem((2 * RADIX * WIDE, 128), F32),
            vmem((2 * RADIX * WIDE, 128), F32),
            table,
            table,
            vmem((N, 128), F32),
            vmem((N, 128), F32),
            vmem((32, 2, 4, 32, 128), BF16),
            vmem((2, 14, 4, 32, 128), BF16),
            vmem((32, 2, 4, 32, 128), BF16),
            vmem((2, 16, 8, HALF), BF16),
            vmem((2, 2, 8, HALF // 2), BF16),
            vmem((2, PLANES, 8, HALF), BF16),
            vmem((2, PLANES, 8, HALF), F32),
            *[vmem((2, PLANES, HALF), BF16)] * 4,
            vmem((8, N), BF16),
            dma((31,)),
            dma((32,)),
            dma((8,)),
            dma((8,)),
            dma((2, 31)),
            dma((32, 2)),
            dma((2, 14)),
            dma((2, 14)),
            dma((2, 14)),
            dma((2, 16, 2)),
            dma((2, 4)),
            dma((2, 2)),
            dma((2, 2)),
            dma((2, 2)),
            dma((20,)),
            dma((4, 4, 2)),
            dma,
        ],
        compiler_params=pltpu.CompilerParams(
            collective_id=0, has_side_effects=True, vmem_limit_bytes=56 << 20
        ),
    )(hologram, background, *pass_tables())
    return merged.reshape(128, N).astype(F32)


def solution(mesh):
    fine = Mesh(mesh.devices.reshape(SIZES), AXES)
    spec = P(("zl", "y", "c"), None)
    return jax.shard_map(
        shards, mesh=fine, in_specs=(spec, spec), out_specs=spec, check_vma=False
    )
```

time: 175 us -> 151 us (0.86)
  Pallas kernels: 164 us -> 148 us
  local copies, waits for them, and re-layouts: 4.53 us -> 0 us
  other arithmetic: 5.7 us -> 2.76 us
    pallas_call x1, Pallas kernels: 164 us -> 148 us  [shards(): pl.pallas_call(whole_kernel, name='whole', out_shape=jax.ShapeDtypeStruct...]
    unnamed x8 -> x0, local copies, waits for them, and re-layouts: 2.53 us -> none
    concatenate x4 -> x0, other arithmetic: 2.07 us -> none  [the longest x2 1.32 us: part(): jnp.concatenate([own, lax.slice_in_dim(table, 32, 33, axis=axis)], axis=a...]
where the time goes in v3:
time: 151 us
  Pallas kernels  148 us (98%)
  other arithmetic  2.76 us (2%)
    pallas_call x1, Pallas kernels, shards(): pl.pallas_call(whole_kernel, name='whole', out_shape=jax.ShapeDtypeStruct...  148 us

profile of v3, /device:TPU:2, one launch (start us, length us, event | category | flops | bytes accessed | tf_op | source)
XLA Modules:
  0.0 151.0 jit_solution(15333811629318326431)
XLA Ops:
  0.0 148.3 %whole.1 = bf16[4,4,8,4096]{3,2,1,0:T(8,128)(2,1)} custom-call(bf16[128,4096]{1,0:T(8,128)(2,1)} %hologram.1, bf16[128,4096]{1,0:T(8,128)(2,1)} %background.1, f32[128,64]{1,0:T(8,128)} %constant.12.clone.open_exact, bf16[128,128]{1,0:T(8,128)(2,1)} %constant.13.clone.ahead, bf16[128,128]{1,0:T(8,128)(2,1)} %constant.14.clone.back, ...), custom_call_target="tpu_custom_call" | custom-call | tf_op jit(solution)/shard_map/whole/pallas_call | solution.py:723
  148.3 2.8 %bitcast_convert_fusion = f32[128,4096]{1,0:T(8,128)} fusion(bf16[4,4,8,4096]{3,2,1,0:T(8,128)(2,1)} %whole.1), kind=kLoop, calls=%fused_computation | loop fusion | flops 524288 | bytes 3145728 | tf_op jit(solution)/shard_map/convert_element_type | solution.py:771

commit v4 on v3

--- a/solution.py
+++ b/solution.py
@@ -14,7 +14,9 @@
 PLANES = 16
 WIDE = 72
 DEEP = 136
-HALF = N // 2
+CHUNKS = 4
+PART = RADIX // CHUNKS
+LANES = N // CHUNKS
 AXES = ("zh", "x", "zl", "y", "c")
 SIZES = (4, 4, 4, 4, 2)
 MESH = pl.DeviceIdType.MESH
@@ -44,7 +46,8 @@
 def pass_tables():
     ahead, back = fourier_tables(-1.0), fourier_tables(1.0)
     flat = lambda table: table.transpose(0, 2, 1, 3).reshape(128, 128)
-    natural = np.eye(128, dtype=np.float32).reshape(2, 2, 32, 128).swapaxes(0, 1).reshape(128, 128)
+    natural = np.eye(128, dtype=np.float32).reshape(2, CHUNKS, PART, 128)
+    natural = natural.swapaxes(0, 1).reshape(128, 128)
     both = np.zeros((2, 2, 2, RADIX, 2, 128), np.float32)
     for lane in range(128):
         far, j = divmod(lane, RADIX)
@@ -90,7 +93,7 @@
         middle[pl.ds(RADIX + b, 16, stride=DEEP), :] = imag * cosine - real * sine
         return carry
 
-    lax.fori_loop(0, RADIX, opening, 0, unroll=8)
+    lax.fori_loop(0, RADIX, opening, 0, unroll=16)
 
     def section(index):
         made = matmul(ahead, middle[index * DEEP : index * DEEP + 128, :].astype(BF16))
@@ -191,7 +194,7 @@
         middle[pl.ds(RADIX + b, RADIX, stride=DEEP), :] = imag * cosine - real * sine
         return carry
 
-    lax.fori_loop(0, RADIX, first, 0, unroll=8)
+    lax.fori_loop(0, RADIX, first, 0, unroll=16)
 
     def second(k, carry):
         made = matmul(ahead, middle[pl.ds(k * DEEP, 128), :].astype(BF16))
@@ -216,7 +219,7 @@
         other[pl.ds(RADIX + k, RADIX, stride=DEEP), :] = real * sine + imag * cosine
         return carry
 
-    lax.fori_loop(0, RADIX, second, 0, unroll=8)
+    lax.fori_loop(0, RADIX, second, 0, unroll=16)
 
     def third(b, carry):
         made = matmul(back, other[pl.ds(b * DEEP, 128), :].astype(BF16))
@@ -224,7 +227,7 @@
         middle[pl.ds(RADIX * WIDE + b, RADIX, stride=WIDE), :] = made[RADIX:]
         return carry
 
-    lax.fori_loop(0, RADIX, third, 0, unroll=8)
+    lax.fori_loop(0, RADIX, third, 0, unroll=16)
 
 
 def block_rows(middle, part, x, yc):
@@ -252,8 +255,8 @@
         cosine, sine = cosines[k], sines[k]
         turned = (real * cosine - imag * sine, real * sine + imag * cosine)
         for part in range(2):
-            for chunk in range(2):
-                rows = turned[part][chunk * 32 : (chunk + 1) * 32]
+            for chunk in range(CHUNKS):
+                rows = turned[part][chunk * PART : (chunk + 1) * PART]
                 blocks[target, chunk, part * 2 + half] = rows.astype(BF16)
 
 
@@ -262,23 +265,24 @@
         for half in range(2):
             k = partner(source) if half else source
             rows = gathered[source, chunk, part * 2 + half].astype(F32)
-            start = chunk * 32 * DEEP + part * RADIX + k
-            other[pl.ds(start, 32, stride=DEEP), :] = rows
+            start = chunk * PART * DEEP + part * RADIX + k
+            other[pl.ds(start, PART, stride=DEEP), :] = rows
 
 
 def close_rows(chunk, back, eye, other, wide, planes):
     def closing(index, carry):
-        b = chunk * 32 + index
+        b = chunk * PART + index
         made = matmul(back, other[pl.ds(b * DEEP, 128), :].astype(BF16))
         real, imag = made[:RADIX], made[RADIX:]
         wide[pl.ds(b, RADIX, stride=WIDE), :] = real * real + imag * imag
         return carry
 
-    lax.fori_loop(0, 32, closing, 0, unroll=8)
-    for t in range(16):
+    lax.fori_loop(0, PART, closing, 0, unroll=PART)
+    span = 128 // PART
+    for t in range(LANES // 128):
         rows = [
-            wide[a * WIDE + chunk * 32 : a * WIDE + chunk * 32 + 32, :]
-            for a in range(4 * t, 4 * t + 4)
+            wide[a * WIDE + chunk * PART : a * WIDE + (chunk + 1) * PART, :]
+            for a in range(span * t, span * (t + 1))
         ]
         block = jnp.concatenate(rows).astype(BF16)
         made = lax.dot_general(eye[...], block, NT, preferred_element_type=F32)
@@ -287,8 +291,8 @@
 
 
 def edge_rows(chunk, stack, low, high):
-    rows = lax.broadcasted_iota(jnp.int32, (PLANES, HALF), 0)
-    bottom, top = jnp.zeros((PLANES, HALF), F32), jnp.zeros((PLANES, HALF), F32)
+    rows = lax.broadcasted_iota(jnp.int32, (PLANES, LANES), 0)
+    bottom, top = jnp.zeros((PLANES, LANES), F32), jnp.zeros((PLANES, LANES), F32)
     for g in range(PLANES):
         plane = stack[chunk, g].astype(F32)
         bottom = jnp.where(rows == g, plane[0:1], bottom)
@@ -308,7 +312,7 @@
 
 
 def row_scores(chunk, stack, scores, north, south, first, last):
-    row = lax.broadcasted_iota(jnp.int32, (8, HALF), 0)
+    row = lax.broadcasted_iota(jnp.int32, (8, LANES), 0)
     norths, souths = north[chunk].astype(F32), south[chunk].astype(F32)
     for g in range(PLANES):
         centre = stack[chunk, g].astype(F32)
@@ -319,34 +323,44 @@
         scores[chunk, g] = scores[chunk, g] + (below - above) * (below - above)
 
 
-def side_scores(stack, scores):
-    lane = lax.broadcasted_iota(jnp.int32, (8, HALF), 1)
-    start, end = lax.rem(lane, 32) == 0, lax.rem(lane, 32) == 31
+def side_scores(chunk, stack, scores):
+    lane = lax.broadcasted_iota(jnp.int32, (8, LANES), 1)
+    start, end = lax.rem(lane, PART) == 0, lax.rem(lane, PART) == PART - 1
 
     def one(g, carry):
-        left, right = stack[0, g].astype(F32), stack[1, g].astype(F32)
-        left_before, left_after = pltpu.roll(left, 1, 1), pltpu.roll(left, HALF - 1, 1)
-        right_before, right_after = pltpu.roll(right, 1, 1), pltpu.roll(right, HALF - 1, 1)
-        west = jnp.where(start, jnp.where(lane == 0, left, right_before), left_before)
-        east = jnp.where(end, pltpu.roll(right, 31, 1), left_after)
-        scores[0, g] = scores[0, g] + (east - west) * (east - west)
-        west = jnp.where(start, pltpu.roll(left, HALF - 31, 1), right_before)
-        east = jnp.where(end, jnp.where(lane == HALF - 1, right, left_after), right_after)
-        scores[1, g] = scores[1, g] + (east - west) * (east - west)
+        centre = stack[chunk, g].astype(F32)
+        before = stack[(chunk - 1) % CHUNKS, g].astype(F32)
+        after = stack[(chunk + 1) % CHUNKS, g].astype(F32)
+        if chunk:
+            before = pltpu.roll(before, LANES - PART + 1, 1)
+        else:
+            before = jnp.where(lane == 0, centre, pltpu.roll(before, 1, 1))
+        if chunk < CHUNKS - 1:
+            after = pltpu.roll(after, PART - 1, 1)
+        else:
+            after = jnp.where(lane == LANES - 1, centre, pltpu.roll(after, LANES - 1, 1))
+        west = jnp.where(start, before, pltpu.roll(centre, 1, 1))
+        east = jnp.where(end, after, pltpu.roll(centre, LANES - 1, 1))
+        scores[chunk, g] = scores[chunk, g] + (east - west) * (east - west)
         return carry
 
-    lax.fori_loop(0, PLANES, one, 0)
+    lax.fori_loop(0, PLANES, one, 0, unroll=2)
 
 
 def sharpest(scores, natural, piece):
-    best = [jnp.max(scores[chunk], axis=0) / 8.0 for chunk in range(2)]
+    best = [jnp.max(scores[chunk], axis=0) / 8.0 for chunk in range(CHUNKS)]
+    width = 128 // CHUNKS
     lane = lax.broadcasted_iota(jnp.int32, (8, 128), 1)
     tiles = []
-    for t in range(16):
-        here = slice(t * 128, (t + 1) * 128)
-        first, second = best[0][:, here], best[1][:, here]
-        tiles.append(jnp.where(lane < RADIX, first, pltpu.roll(second, RADIX, 1)))
-        tiles.append(jnp.where(lane < RADIX, pltpu.roll(first, RADIX, 1), second))
+    for t in range(32):
+        here = slice(t // CHUNKS * 128, (t // CHUNKS + 1) * 128)
+        made = jnp.zeros((8, 128), F32)
+        for chunk in range(CHUNKS):
+            shift = (chunk - t) % CHUNKS * width
+            moved = best[chunk][:, here]
+            moved = pltpu.roll(moved, shift, 1) if shift else moved
+            made = jnp.where(lane // width == chunk, moved, made)
+        tiles.append(made)
     made = matmul_right(jnp.concatenate(tiles).astype(BF16), natural)
     for t in range(32):
         piece[:, t * 128 : (t + 1) * 128] = made[t * 8 : (t + 1) * 8].astype(BF16)
@@ -437,8 +451,10 @@
     everyone += [ahead_q, behind_q]
     for device in everyone:
         pl.semaphore_signal(barrier, inc=1, device_id=device, device_id_type=MESH)
-    row_pass(x, hologram, background, open_exact, ahead, eye, wide, middle, sections)
-    pl.semaphore_wait(barrier, len(everyone))
+    with jax.named_scope("row_pass"):
+        row_pass(x, hologram, background, open_exact, ahead, eye, wide, middle, sections)
+    with jax.named_scope("barrier"):
+        pl.semaphore_wait(barrier, len(everyone))
 
     sent = []
     for index, (side, dc, turn) in enumerate(hops):
@@ -467,7 +483,8 @@
         sent[-1].start()
     own = pltpu.make_async_copy(sections.at[yc], columns.at[slab], own_sem)
     own.start()
-    make_tables(me, z, cosines, sines, k_real, k_imag)
+    with jax.named_scope("tables"):
+        make_tables(me, z, cosines, sines, k_real, k_imag)
     own.wait()
     widen(slab, columns, wide)
     for index, (side, dc, turn) in enumerate(hops):
@@ -496,7 +513,8 @@
         copy.wait_send()
 
     tables = (open_exact, ahead, back)
-    column_pass(me, tables, wide, middle, other, k_real, k_imag, cosines, sines)
+    with jax.named_scope("column_pass"):
+        column_pass(me, tables, wide, middle, other, k_real, k_imag, cosines, sines)
 
     sent = []
 
@@ -540,10 +558,11 @@
             send_direct(0, index - 1)
             send_direct(0, index)
     send_direct(0, len(direct) - 1)
-    for index in range(len(relayed)):
-        send_relayed(1, index)
-    for index in range(len(direct)):
-        send_direct(1, index)
+    for chunk in range(1, CHUNKS):
+        for index in range(len(relayed)):
+            send_relayed(chunk, index)
+        for index in range(len(direct)):
+            send_direct(chunk, index)
     make(level(0, 0, 0))
     own = pltpu.make_async_copy(blocks.at[me], gathered.at[me], own_sem)
     own.start()
@@ -552,7 +571,7 @@
     def part(chunk, layer):
         return planes.at[chunk, lax.rem(layer, 4) * 4 + layer // 4]
 
-    lanes = (pl.ds(0, HALF // 2), pl.ds(HALF // 2, HALF // 2))
+    lanes = (pl.ds(0, LANES // 2), pl.ds(LANES // 2, LANES // 2))
 
     def forward_far(chunk):
         for side, turn in enumerate((4, -4)):
@@ -569,7 +588,7 @@
             )
             sent[-1].start()
 
-    for chunk in range(2):
+    for chunk in range(CHUNKS):
         for index, (hx, hy, dc, rx, ry) in enumerate(relayed):
             source = level(-hx, -hy, dc)
             slot = staged.at[chunk, index]
@@ -593,9 +612,10 @@
             slot = gathered.at[source, chunk]
             remote(slot, slot, own_sem, recv2.at[source, chunk], device).wait_recv()
             place_block(source, chunk, gathered, other)
-        close_rows(chunk, back, eye, other, wide, planes)
+        with jax.named_scope(f"close{chunk}"):
+            close_rows(chunk, back, eye, other, wide, planes)
         if chunk:
-            forward_far(0)
+            forward_far(chunk - 1)
         far = up(8)
         for side, turn in enumerate((4, -4)):
             sent.append(
@@ -623,7 +643,7 @@
         own = pltpu.make_async_copy(part(chunk, z), stack.at[chunk, z], own_sem)
         own.start()
         own.wait()
-    forward_far(1)
+    forward_far(CHUNKS - 1)
 
     def edges(chunk):
         edge_rows(chunk, stack, low, high)
@@ -641,23 +661,29 @@
             copy.start()
         return pair
 
-    for chunk in range(2):
+    for chunk in range(CHUNKS):
         for turn in reversed(turns):
             slot = stack.at[chunk, up(turn)]
             remote(slot, slot, own_sem, recv3.at[chunk, up(turn), 0], above(up(turn))).wait_recv()
         for side, turn in enumerate((-4, 4)):
             slot = stack.at[chunk, up(8), :, lanes[side]]
             remote(slot, slot, own_sem, recv3.at[chunk, up(8), side], above(up(turn))).wait_recv()
-        pair = edges(chunk)
-        depth_scores(chunk, stack, scores)
-        if chunk:
-            side_scores(stack, scores)
+        with jax.named_scope(f"depth{chunk}"):
+            pair = edges(chunk)
+            depth_scores(chunk, stack, scores)
+        if chunk > 1:
+            side_scores(chunk - 1, stack, scores)
+        if chunk == CHUNKS - 1:
+            side_scores(0, stack, scores)
+            side_scores(chunk, stack, scores)
         for copy in pair:
             copy.wait()
-        row_scores(chunk, stack, scores, north, south, q == 0, q == 511)
+        with jax.named_scope(f"rows{chunk}"):
+            row_scores(chunk, stack, scores, north, south, q == 0, q == 511)
     for copy in sent:
         copy.wait_send()
-    sharpest(scores, natural, piece)
+    with jax.named_scope("sharpest"):
+        sharpest(scores, natural, piece)
 
     left, right = pl.ds(0, N // 2), pl.ds(N // 2, N // 2)
     halves = (left, right)
@@ -737,35 +763,35 @@
             table,
             vmem((N, 128), F32),
             vmem((N, 128), F32),
-            vmem((32, 2, 4, 32, 128), BF16),
-            vmem((2, 14, 4, 32, 128), BF16),
-            vmem((32, 2, 4, 32, 128), BF16),
-            vmem((2, 16, 8, HALF), BF16),
-            vmem((2, 2, 8, HALF // 2), BF16),
-            vmem((2, PLANES, 8, HALF), BF16),
-            vmem((2, PLANES, 8, HALF), F32),
-            *[vmem((2, PLANES, HALF), BF16)] * 4,
+            vmem((32, CHUNKS, 4, PART, 128), BF16),
+            vmem((CHUNKS, 14, 4, PART, 128), BF16),
+            vmem((32, CHUNKS, 4, PART, 128), BF16),
+            vmem((CHUNKS, 16, 8, LANES), BF16),
+            vmem((CHUNKS, 2, 8, LANES // 2), BF16),
+            vmem((CHUNKS, PLANES, 8, LANES), BF16),
+            vmem((CHUNKS, PLANES, 8, LANES), F32),
+            *[vmem((CHUNKS, PLANES, LANES), BF16)] * 4,
             vmem((8, N), BF16),
             dma((31,)),
             dma((32,)),
             dma((8,)),
             dma((8,)),
-            dma((2, 31)),
-            dma((32, 2)),
-            dma((2, 14)),
-            dma((2, 14)),
-            dma((2, 14)),
-            dma((2, 16, 2)),
-            dma((2, 4)),
-            dma((2, 2)),
-            dma((2, 2)),
-            dma((2, 2)),
+            dma((CHUNKS, 31)),
+            dma((32, CHUNKS)),
+            dma((CHUNKS, 14)),
+            dma((CHUNKS, 14)),
+            dma((CHUNKS, 14)),
+            dma((CHUNKS, 16, 2)),
+            dma((CHUNKS, 4)),
+            dma((CHUNKS, 2)),
+            dma((CHUNKS, 2)),
+            dma((CHUNKS, 2)),
             dma((20,)),
             dma((4, 4, 2)),
             dma,
         ],
         compiler_params=pltpu.CompilerParams(
-            collective_id=0, has_side_effects=True, vmem_limit_bytes=56 << 20
+            collective_id=0, has_side_effects=True, vmem_limit_bytes=44 << 20
         ),
     )(hologram, background, *pass_tables())
     return merged.reshape(128, N).astype(F32)

time: 151 us -> 167 us (1.11)
  the two profiles are of different devices: /device:TPU:2 before, /device:TPU:98 now
where the time goes in v4:
time: 167 us; the launch traced here: 166 us
  Pallas kernels  158 us (95%)
  local copies, waits for them, and re-layouts  7.27 us (4%)
    pallas_call x1, Pallas kernels, shards(): pl.pallas_call(whole_kernel, name='whole', out_shape=jax.ShapeDtypeStruct...  158 us
    unnamed x16, local copies, waits for them, and re-layouts  7.27 us

profile of v4, /device:TPU:98, one launch (start us, length us, event | category | flops | bytes accessed | tf_op | source)
XLA Modules:
  0.0 166.4 jit_solution(16143428071428923158)
XLA Ops:
  0.0 0.0 copy-start
  0.0 1.2 copy-done
  1.2 0.0 copy-start.1
  1.2 1.2 copy-done.1
  2.5 0.0 copy-start.2
  2.5 0.9 copy-done.2
  3.4 0.0 copy-start.3
  3.4 0.8 copy-done.3
  4.2 0.0 copy-start.4
  4.2 0.8 copy-done.4
  5.0 0.0 copy-start.5
  5.0 0.8 copy-done.5
  5.8 0.0 copy-start.6
  5.8 0.8 copy-done.6
  6.5 0.0 copy-start.7
  6.5 0.8 copy-done.7
  7.3 157.6 %whole.1 = bf16[4,4,8,4096]{3,2,1,0:T(8,128)(2,1)S(1)} custom-call(bf16[128,4096]{1,0:T(8,128)(2,1)S(1)} %copy-done, bf16[128,4096]{1,0:T(8,128)(2,1)S(1)} %copy-done.1, f32[128,64]{1,0:T(8,128)S(1)} %copy-done.3, bf16[128,128]{1,0:T(8,128)(2,1)S(1)} %copy-done.7, bf16[128,128]{1,0:T(8,128)(2,1)S(1)} %copy-done.6, bf16[2,256,256]{2,1,0:T(8,128)(2,1)S(1)} %copy-done.2, ...), custom_call_target="tpu_custom_call" | custom-call | tf_op jit(solution)/shard_map/whole/pallas_call | solution.py:749
  164.8 1.6 bitcast_convert_fusion
Async XLA Ops:
  0.0 1.2 copy-start
  1.2 1.2 copy-start.1
  2.5 0.9 copy-start.2
  3.4 0.8 copy-start.3
  4.2 0.8 copy-start.4
  5.0 0.8 copy-start.5
  5.8 0.8 copy-start.6
  6.5 0.8 copy-start.7

commit v5 on v4

--- a/solution.py
+++ b/solution.py
@@ -14,7 +14,7 @@
 PLANES = 16
 WIDE = 72
 DEEP = 136
-CHUNKS = 4
+CHUNKS = 2
 PART = RADIX // CHUNKS
 LANES = N // CHUNKS
 AXES = ("zh", "x", "zl", "y", "c")
@@ -277,7 +277,7 @@
         wide[pl.ds(b, RADIX, stride=WIDE), :] = real * real + imag * imag
         return carry
 
-    lax.fori_loop(0, PART, closing, 0, unroll=PART)
+    lax.fori_loop(0, PART, closing, 0, unroll=16)
     span = 128 // PART
     for t in range(LANES // 128):
         rows = [
@@ -367,7 +367,8 @@
 
 
 def whole_kernel(
-    hologram, background, open_exact, ahead, back, both, eye, natural, out,
+    hologram_in, background_in, exact_in, ahead_in, back_in, both_in, eye_in, natural_in, out,
+    hologram, background, open_exact, ahead, back, both, eye, natural, load_sem,
     sections, columns, passing, wide, middle, other, cosines, sines, k_real, k_imag,
     blocks, staged, gathered, planes, opposite, stack, scores, low, high, north, south, piece,
     send1, recv1, relay1_send, relay1_recv, send2, recv2, relay_send, relay_recv,
@@ -444,6 +445,17 @@
     turns = (7, -7, 6, -6, 5, -5, 4, -4, 3, -3, 2, -2, 1, -1)
     ahead_q, behind_q = block_owner(lax.rem(q + 1, 512)), block_owner(lax.rem(q + 511, 512))
 
+    pairs = (
+        (hologram_in, hologram), (background_in, background), (eye_in, eye),
+        (exact_in, open_exact), (ahead_in, ahead), (back_in, back), (both_in, both),
+        (natural_in, natural),
+    )
+    loads = [
+        pltpu.make_async_copy(source, target, load_sem.at[index])
+        for index, (source, target) in enumerate(pairs)
+    ]
+    for copy in loads:
+        copy.start()
     barrier = pltpu.get_barrier_semaphore()
     everyone = [near(-dy, dc, -turn) for dy, dc, turn in moves + hops]
     everyone += [level(dx, dy, dc) for dx in range(4) for dy in range(4) for dc in range(2)][1:]
@@ -451,10 +463,10 @@
     everyone += [ahead_q, behind_q]
     for device in everyone:
         pl.semaphore_signal(barrier, inc=1, device_id=device, device_id_type=MESH)
-    with jax.named_scope("row_pass"):
-        row_pass(x, hologram, background, open_exact, ahead, eye, wide, middle, sections)
-    with jax.named_scope("barrier"):
-        pl.semaphore_wait(barrier, len(everyone))
+    for copy in loads:
+        copy.wait()
+    row_pass(x, hologram, background, open_exact, ahead, eye, wide, middle, sections)
+    pl.semaphore_wait(barrier, len(everyone))
 
     sent = []
     for index, (side, dc, turn) in enumerate(hops):
@@ -483,8 +495,7 @@
         sent[-1].start()
     own = pltpu.make_async_copy(sections.at[yc], columns.at[slab], own_sem)
     own.start()
-    with jax.named_scope("tables"):
-        make_tables(me, z, cosines, sines, k_real, k_imag)
+    make_tables(me, z, cosines, sines, k_real, k_imag)
     own.wait()
     widen(slab, columns, wide)
     for index, (side, dc, turn) in enumerate(hops):
@@ -513,8 +524,7 @@
         copy.wait_send()
 
     tables = (open_exact, ahead, back)
-    with jax.named_scope("column_pass"):
-        column_pass(me, tables, wide, middle, other, k_real, k_imag, cosines, sines)
+    column_pass(me, tables, wide, middle, other, k_real, k_imag, cosines, sines)
 
     sent = []
 
@@ -558,11 +568,6 @@
             send_direct(0, index - 1)
             send_direct(0, index)
     send_direct(0, len(direct) - 1)
-    for chunk in range(1, CHUNKS):
-        for index in range(len(relayed)):
-            send_relayed(chunk, index)
-        for index in range(len(direct)):
-            send_direct(chunk, index)
     make(level(0, 0, 0))
     own = pltpu.make_async_copy(blocks.at[me], gathered.at[me], own_sem)
     own.start()
@@ -603,6 +608,11 @@
                 )
             )
             sent[-1].start()
+        if chunk + 1 < CHUNKS:
+            for index in range(len(relayed)):
+                send_relayed(chunk + 1, index)
+            for index in range(len(direct)):
+                send_direct(chunk + 1, index)
         place_block(me, chunk, gathered, other)
         arrivals = [(-dx, -dy, dc) for dx, dy, dc in direct]
         arrivals += [(-hx - rx, -hy - ry, dc) for hx, hy, dc, rx, ry in relayed]
@@ -612,8 +622,7 @@
             slot = gathered.at[source, chunk]
             remote(slot, slot, own_sem, recv2.at[source, chunk], device).wait_recv()
             place_block(source, chunk, gathered, other)
-        with jax.named_scope(f"close{chunk}"):
-            close_rows(chunk, back, eye, other, wide, planes)
+        close_rows(chunk, back, eye, other, wide, planes)
         if chunk:
             forward_far(chunk - 1)
         far = up(8)
@@ -668,9 +677,8 @@
         for side, turn in enumerate((-4, 4)):
             slot = stack.at[chunk, up(8), :, lanes[side]]
             remote(slot, slot, own_sem, recv3.at[chunk, up(8), side], above(up(turn))).wait_recv()
-        with jax.named_scope(f"depth{chunk}"):
-            pair = edges(chunk)
-            depth_scores(chunk, stack, scores)
+        pair = edges(chunk)
+        depth_scores(chunk, stack, scores)
         if chunk > 1:
             side_scores(chunk - 1, stack, scores)
         if chunk == CHUNKS - 1:
@@ -678,12 +686,10 @@
             side_scores(chunk, stack, scores)
         for copy in pair:
             copy.wait()
-        with jax.named_scope(f"rows{chunk}"):
-            row_scores(chunk, stack, scores, north, south, q == 0, q == 511)
+        row_scores(chunk, stack, scores, north, south, q == 0, q == 511)
     for copy in sent:
         copy.wait_send()
-    with jax.named_scope("sharpest"):
-        sharpest(scores, natural, piece)
+    sharpest(scores, natural, piece)
 
     left, right = pl.ds(0, N // 2), pl.ds(N // 2, N // 2)
     halves = (left, right)
@@ -750,9 +756,18 @@
         whole_kernel,
         name="whole",
         out_shape=jax.ShapeDtypeStruct((4, 4, 8, N), BF16),
-        in_specs=[pl.BlockSpec(memory_space=vmem)] * 8,
+        in_specs=[pl.BlockSpec(memory_space=pltpu.HBM)] * 8,
         out_specs=pl.BlockSpec(memory_space=vmem),
         scratch_shapes=[
+            vmem((128, N), BF16),
+            vmem((128, N), BF16),
+            vmem((128, RADIX), F32),
+            vmem((128, 128), BF16),
+            vmem((128, 128), BF16),
+            vmem((2, 256, 256), BF16),
+            vmem((128, 128), BF16),
+            vmem((128, 128), BF16),
+            dma((8,)),
             vmem((8, 128, 128), BF16),
             vmem((32, 128, 128), BF16),
             vmem((8, 128, 128), BF16),
@@ -791,7 +806,7 @@
             dma,
         ],
         compiler_params=pltpu.CompilerParams(
-            collective_id=0, has_side_effects=True, vmem_limit_bytes=44 << 20
+            collective_id=0, has_side_effects=True, vmem_limit_bytes=65400000
         ),
     )(hologram, background, *pass_tables())
     return merged.reshape(128, N).astype(F32)

time: 167 us -> 140 us (0.84)
  the two profiles are of different devices: /device:TPU:98 before, /device:TPU:2 now
where the time goes in v5:
time: 140 us
  Pallas kernels  137 us (98%)
  other arithmetic  2.76 us (2%)
    pallas_call x1, Pallas kernels, shards(): pl.pallas_call(whole_kernel, name='whole', out_shape=jax.ShapeDtypeStruct...  137 us

profile of v5, /device:TPU:2, one launch (start us, length us, event | category | flops | bytes accessed | tf_op | source)
XLA Modules:
  0.0 139.9 jit_solution(3922278533537715554)
XLA Ops:
  0.0 137.1 %whole.1 = bf16[4,4,8,4096]{3,2,1,0:T(8,128)(2,1)} custom-call(bf16[128,4096]{1,0:T(8,128)(2,1)} %hologram_in.1, bf16[128,4096]{1,0:T(8,128)(2,1)} %background_in.1, f32[128,64]{1,0:T(8,128)} %constant.12.clone.exact_in, bf16[128,128]{1,0:T(8,128)(2,1)} %constant.13.clone.ahead_in, bf16[128,128]{1,0:T(8,128)(2,1)} %constant.14.clone.back_in, ...), custom_call_target="tpu_custom_call" | custom-call | tf_op jit(solution)/shard_map/whole/pallas_call | solution.py:755
  137.1 2.8 %bitcast_convert_fusion = f32[128,4096]{1,0:T(8,128)} fusion(bf16[4,4,8,4096]{3,2,1,0:T(8,128)(2,1)} %whole.1), kind=kLoop, calls=%fused_computation | loop fusion | flops 524288 | bytes 3145728 | tf_op jit(solution)/shard_map/convert_element_type | solution.py:812

commit v6 on v5

--- a/solution.py
+++ b/solution.py
@@ -14,7 +14,7 @@
 PLANES = 16
 WIDE = 72
 DEEP = 136
-CHUNKS = 2
+CHUNKS = 4
 PART = RADIX // CHUNKS
 LANES = N // CHUNKS
 AXES = ("zh", "x", "zl", "y", "c")

time: 140 us -> 152 us (1.086)
  the two profiles are of different devices: /device:TPU:2 before, /device:TPU:4 now
where the time goes in v6:
time: 152 us
  Pallas kernels  149 us (98%)
  other arithmetic  2.76 us (2%)
    pallas_call x1, Pallas kernels, shards(): pl.pallas_call(whole_kernel, name='whole', out_shape=jax.ShapeDtypeStruct...  149 us

profile of v6, /device:TPU:4, one launch (start us, length us, event | category | flops | bytes accessed | tf_op | source)
XLA Modules:
  0.0 151.8 jit_solution(6062104625536758514)
XLA Ops:
  0.0 149.0 %whole.1 = bf16[4,4,8,4096]{3,2,1,0:T(8,128)(2,1)} custom-call(bf16[128,4096]{1,0:T(8,128)(2,1)} %hologram_in.1, bf16[128,4096]{1,0:T(8,128)(2,1)} %background_in.1, f32[128,64]{1,0:T(8,128)} %constant.12.clone.exact_in, bf16[128,128]{1,0:T(8,128)(2,1)} %constant.13.clone.ahead_in, bf16[128,128]{1,0:T(8,128)(2,1)} %constant.14.clone.back_in, ...), custom_call_target="tpu_custom_call" | custom-call | tf_op jit(solution)/shard_map/whole/pallas_call | solution.py:755
  149.0 2.8 %bitcast_convert_fusion = f32[128,4096]{1,0:T(8,128)} fusion(bf16[4,4,8,4096]{3,2,1,0:T(8,128)(2,1)} %whole.1), kind=kLoop, calls=%fused_computation | loop fusion | flops 524288 | bytes 3145728 | tf_op jit(solution)/shard_map/convert_element_type | solution.py:812

commit v7 on v5

--- a/solution.py
+++ b/solution.py
@@ -442,6 +442,7 @@
                     relayed.append((hop[0], hop[1], dc, rest[0], rest[1]))
                 elif (dx, dy, dc) != (0, 0, 0):
                     direct.append((-1 if dx == 3 else dx, -1 if dy == 3 else dy, dc))
+    distant = [(hx + rx, hy + ry, dc) for hx, hy, dc, rx, ry in relayed]
     turns = (7, -7, 6, -6, 5, -5, 4, -4, 3, -3, 2, -2, 1, -1)
     ahead_q, behind_q = block_owner(lax.rem(q + 1, 512)), block_owner(lax.rem(q + 511, 512))
 
@@ -542,7 +543,7 @@
         sent[-1].start()
 
     def send_direct(chunk, index):
-        device = level(*direct[index])
+        device = level(*(direct + distant)[index])
         sent.append(
             remote(
                 blocks.at[number(device), chunk],
@@ -594,7 +595,7 @@
             sent[-1].start()
 
     for chunk in range(CHUNKS):
-        for index, (hx, hy, dc, rx, ry) in enumerate(relayed):
+        for index, (hx, hy, dc, rx, ry) in enumerate(relayed if chunk == 0 else []):
             source = level(-hx, -hy, dc)
             slot = staged.at[chunk, index]
             remote(slot, slot, own_sem, relay_recv.at[chunk, index], source).wait_recv()
@@ -609,9 +610,7 @@
             )
             sent[-1].start()
         if chunk + 1 < CHUNKS:
-            for index in range(len(relayed)):
-                send_relayed(chunk + 1, index)
-            for index in range(len(direct)):
+            for index in reversed(range(len(direct + distant))):
                 send_direct(chunk + 1, index)
         place_block(me, chunk, gathered, other)
         arrivals = [(-dx, -dy, dc) for dx, dy, dc in direct]

time: 140 us -> 145 us (1.036)
  the two profiles are of different devices: /device:TPU:2 before, /device:TPU:8 now
where the time goes in v7:
time: 145 us
  Pallas kernels  142 us (98%)
  other arithmetic  2.76 us (2%)
    pallas_call x1, Pallas kernels, shards(): pl.pallas_call(whole_kernel, name='whole', out_shape=jax.ShapeDtypeStruct...  142 us

profile of v7, /device:TPU:8, one launch (start us, length us, event | category | flops | bytes accessed | tf_op | source)
XLA Modules:
  0.0 144.6 jit_solution(7074591064850512592)
XLA Ops:
  0.0 141.9 %whole.1 = bf16[4,4,8,4096]{3,2,1,0:T(8,128)(2,1)} custom-call(bf16[128,4096]{1,0:T(8,128)(2,1)} %hologram_in.1, bf16[128,4096]{1,0:T(8,128)(2,1)} %background_in.1, f32[128,64]{1,0:T(8,128)} %constant.12.clone.exact_in, bf16[128,128]{1,0:T(8,128)(2,1)} %constant.13.clone.ahead_in, bf16[128,128]{1,0:T(8,128)(2,1)} %constant.14.clone.back_in, ...), custom_call_target="tpu_custom_call" | custom-call | tf_op jit(solution)/shard_map/whole/pallas_call | solution.py:754
  141.9 2.8 %bitcast_convert_fusion = f32[128,4096]{1,0:T(8,128)} fusion(bf16[4,4,8,4096]{3,2,1,0:T(8,128)(2,1)} %whole.1), kind=kLoop, calls=%fused_computation | loop fusion | flops 524288 | bytes 3145728 | tf_op jit(solution)/shard_map/convert_element_type | solution.py:811
